TPU v7x, 32 devices: a whole 2x2x4 slice. The times are simulated.
32 devices in a mesh: prow: 4 (over z), pcol: 8 (over y, x, core).
Axes of the slice: x: 2, y: 2, z: 4, core: 2. Of those that a mesh axis runs over, the one named last changes fastest.
Arguments:
- blocks: bfloat16 [2048, 64, 128], P(('prow', 'pcol')), may hold values from -6 to 6
- owner: int32 [2048, 1], P(('prow', 'pcol')), may hold values from 0 to 31; in each aligned block of 64 rows (0 to 63, 64 to 127, ...) at most 2 rows name the same one
- row_offset: int32 [2048], P(('prow', 'pcol')), may hold values from 0 to 320
- col_offset: int32 [2048], P(('prow', 'pcol')), may hold values from 0 to 256
- exposure: int32 [2048], P(('prow', 'pcol')), may hold values from 0 to 255
- basis_rows: bfloat16 [21, 31], replicated, may hold values from -1 to 1
- basis_cols: bfloat16 [21, 31], replicated, may hold values from -1 to 1
- coef_table: float32 [256, 21], replicated, may hold values from -1.25 to 1.25
- weight_table: float32 [256], replicated, may hold values from 0.2 to 2
- det_taps: float32 [31], replicated, may hold values from 0.02 to 0.12
Outputs:
- coadd: float32 [1536, 3072], P('prow', 'pcol')
- detection: float32 [1536, 3072], P('prow', 'pcol')
Inputs may be any that keep to these rules, and one draw needn't show every extreme that they name: The blocks of one device name one owner at most 2 times; some device names some owner exactly 2 times.
All inputs are finite; a program needn't handle non-finite values.
Results may differ from a plain program's by a relative error of at most 0.009.
Values may be sent and summed in bfloat16 or wider, within the bound.
A program may use at most 192 MiB of HBM per device.

v0:
```python
import math

import jax
import jax.numpy as jnp
from jax import lax
from jax.sharding import PartitionSpec as P

DET_R = 15
PATCH = 384
CAP = 2


def padded_2(value, sides, width):
    for axis, dim in sides:
        size, length = (lax.axis_size(axis), value.shape[dim])
        up = [(i, (i + 1) % size) for i in range(size - 1)]
        down = [(j, i) for i, j in up]
        last = lax.slice_in_dim(value, length - width, length, axis=dim)
        leading = lax.slice_in_dim(value, 0, width, axis=dim)
        before = lax.ppermute(last, axis, up)
        after = lax.ppermute(leading, axis, down)
        value = jnp.concatenate([before, value, after], axis=dim)
    return value


def lookup(indices, table):
    hits = (indices[:, None] == jnp.arange(table.shape[0])[None, :]).astype(jnp.float32)
    return jnp.dot(hits, table, precision=lax.Precision.HIGHEST)


def match_blocks(pixels, coefs, basis_rows, basis_cols, live):
    count, rows, cols = pixels.shape
    kinds, length = basis_rows.shape
    half = length // 2
    group = math.gcd(count, 64)
    taps = jnp.arange(length)
    cols_in = jnp.arange(cols)
    rows_in = jnp.arange(rows)
    col_hits = (
        cols_in[:, None, None] - cols_in[None, :, None] + half == taps[None, None, :]
    ).astype(jnp.float32)
    col_table = jnp.sum(
        col_hits[:, None, :, :] * basis_cols.astype(jnp.float32)[None, :, None, :], axis=3
    ).astype(jnp.bfloat16)
    col_table = col_table.reshape(cols, kinds * cols)
    row_hits = (
        rows_in[None, :, None] - rows_in[:, None, None] + half == taps[None, None, :]
    ).astype(jnp.bfloat16)

    def compute(operand):
        piece, coef = operand
        section = jnp.dot(
            piece.reshape(group * rows, cols), col_table, preferred_element_type=jnp.float32
        )
        section = section.astype(jnp.bfloat16).reshape(group, rows, kinds, cols)
        scaled = (coef[:, :, None] * basis_rows.astype(jnp.float32)[None]).astype(jnp.bfloat16)
        row_table = jnp.einsum(
            "rat,gkt->grka", row_hits, scaled, preferred_element_type=jnp.float32
        ).astype(jnp.bfloat16)
        return jnp.einsum(
            "grka,gakc->grc", row_table, section, preferred_element_type=jnp.float32
        ).astype(jnp.bfloat16)

    def skipped(operand):
        return jnp.zeros((group, rows, cols), jnp.bfloat16)

    def one(args):
        number, piece, coef = args
        return lax.cond(number * group < live, compute, skipped, (piece, coef))

    numbers = jnp.arange(count // group, dtype=jnp.int32)
    done = lax.map(
        one,
        (
            numbers,
            pixels.reshape(count // group, group, rows, cols),
            coefs.reshape(count // group, group, kinds),
        ),
    )
    return done.reshape(count, rows, cols)


def shards(
    blocks,
    owner,
    row_offset,
    col_offset,
    exposure,
    basis_rows,
    basis_cols,
    coef_table,
    weight_table,
    det_taps,
):
    nrow = lax.axis_size("prow")
    ncol = lax.axis_size("pcol")
    owners = nrow * ncol
    count, rows, cols = blocks.shape
    dest = owner[:, 0]
    hits = (dest[:, None] == jnp.arange(owners)[None, :]).astype(jnp.int32)
    rank = jnp.sum((jnp.cumsum(hits, axis=0) - hits) * hits, axis=1)
    slot = dest * CAP + rank
    outgoing = jnp.zeros((owners * CAP, rows, cols), jnp.bfloat16).at[slot].set(blocks)
    labels = jnp.stack([jnp.ones_like(exposure), exposure, row_offset, col_offset], axis=1)
    info_out = jnp.zeros((owners * CAP, 4), jnp.int32).at[slot].set(labels)
    arrived = lax.all_to_all(
        outgoing.reshape(owners, CAP, rows, cols),
        ("prow", "pcol"),
        split_axis=0,
        concat_axis=0,
        tiled=True,
    )
    info = lax.all_to_all(
        info_out.reshape(owners, CAP, 4), ("prow", "pcol"), split_axis=0, concat_axis=0, tiled=True
    )
    flat_info = info.reshape(-1, 4)
    flat_pixels = arrived.reshape(-1, rows, cols)
    occupied = flat_info[:, 0]
    order = jnp.argsort(1 - occupied, stable=True)
    live = jnp.sum(occupied)
    packed = match_blocks(
        flat_pixels[order], lookup(flat_info[order, 1], coef_table), basis_rows, basis_cols, live
    )
    flat = jnp.zeros_like(flat_pixels).at[order].set(packed)
    arrived = flat.reshape(arrived.shape)
    arrived, info = (arrived, info)
    matched = arrived.reshape(owners * CAP, rows, cols)
    info = info.reshape(owners * CAP, 4)
    exposure_weight = (
        lookup(info[:, 1], weight_table[:, None])[:, 0].astype(jnp.bfloat16).astype(jnp.float32)
    )
    weights = exposure_weight * info[:, 0].astype(jnp.float32)
    weighted = (weights[:, None, None] * matched.astype(jnp.float32)).astype(jnp.bfloat16)
    span = jnp.arange(PATCH)
    first_row = info[:, 2]
    first_col = info[:, 3]
    col_pick = (
        first_col[:, None, None] + jnp.arange(cols)[None, :, None] == span[None, None, :]
    ).astype(jnp.bfloat16)
    shifted = jnp.einsum(
        "sab,sbc->sac", weighted, col_pick, preferred_element_type=jnp.float32
    ).astype(jnp.bfloat16)
    row_pick = (
        first_row[None, :, None] + jnp.arange(rows)[None, None, :] == span[:, None, None]
    ).astype(jnp.bfloat16)
    total = jnp.einsum("rsa,sac->rc", row_pick, shifted, preferred_element_type=jnp.float32)
    row_cover = (
        (span[None, :] >= first_row[:, None]) & (span[None, :] < first_row[:, None] + rows)
    ).astype(jnp.float32)
    col_cover = (
        (span[None, :] >= first_col[:, None]) & (span[None, :] < first_col[:, None] + cols)
    ).astype(jnp.bfloat16)
    row_weight = (weights[:, None] * row_cover).astype(jnp.bfloat16)
    depth = jnp.dot(row_weight.T, col_cover, preferred_element_type=jnp.float32)
    coadd = total / jnp.maximum(depth, 1.0)
    padded = padded_2(coadd, (("prow", 0), ("pcol", 1)), DET_R)
    wide = jnp.arange(PATCH + 2 * DET_R)
    reach = jnp.arange(2 * DET_R + 1)
    band_hits = (wide[None, :, None] - span[:, None, None] == reach[None, None, :]).astype(
        jnp.float32
    )
    band = jnp.sum(band_hits * det_taps[None, None, :], axis=2)
    across = jnp.dot(band, padded, precision=lax.Precision.HIGHEST)
    detection = jnp.dot(across, band.T, precision=lax.Precision.HIGHEST)
    return (coadd, detection)


def solution(mesh):
    in_specs = (
        P(("prow", "pcol"), None, None),
        P(("prow", "pcol"), None),
        P(("prow", "pcol")),
        P(("prow", "pcol")),
        P(("prow", "pcol")),
        P(),
        P(),
        P(),
        P(),
        P(),
    )
    out_specs = (P("prow", "pcol"), P("prow", "pcol"))
    return jax.shard_map(shards, mesh=mesh, in_specs=in_specs, out_specs=out_specs, check_vma=False)
```

profile of v0, /device:TPU:1, one launch (start us, length us, event | category | flops | bytes accessed | tf_op | source)
XLA Modules:
  0.0 198.4 jit_solution(6634619709020479171)
XLA Ops:
  0.6 0.0 copy-start
  0.6 0.7 fusion.49
  1.4 0.1 reduce_window_sum.11
  1.5 0.8 select_reduce_fusion.1
  2.3 0.7 fusion.52
  3.0 0.7 pad_add_fusion
  3.7 0.1 copy.33
  3.8 1.3 scatter_custom_fusion
  5.1 7.1 %all-to-all-start = ((s32[32,2,4]{2,1,0:T(2,128)}), s32[32,2,4]{2,1,0:T(2,128)S(1)}, u32[]{:S(2)}, u32[]{:S(2)}) async-start(s32[32,2,4]{2,1,0:T(2,128)} %bitcast.17), calls=%async_computation | async-start | bytes 65536 | tf_op jit(solution)/shard_map/all_to_all | solution.py:113
  12.2 0.2 fusion.18
  12.5 1.2 broadcast.116.clone
  13.7 9.1 %scatter_fusion = bf16[64,64,128]{2,1,0:T(8,128)(2,1)} fusion(bf16[64,64,128]{2,1,0:T(8,128)(2,1)} %broadcast.116.clone, s32[64]{0:T(128)S(1)} %fusion.52, bf16[64,64,128]{2,1,0:T(8,128)(2,1)} %param.12), kind=kCustom, calls=%fused_computation.3 | custom fusion | bytes 3145984 | tf_op jit(solution)/shard_map/scatter | solution.py:103
  22.8 0.0 all-to-all-done
  22.8 5.8 %all-to-all-start.1 = ((bf16[32,2,64,128]{3,2,1,0:T(8,128)(2,1)}), bf16[32,2,64,128]{3,2,1,0:T(8,128)(2,1)S(1)}, u32[]{:S(2)}, u32[]{:S(2)}) async-start(bf16[32,2,64,128]{3,2,1,0:T(8,128)(2,1)} %bitcast.26), calls=%async_computation.1 | async-start | bytes 2097152 | tf_op jit(solution)/shard_map/all_to_all | solution.py:106
  28.6 0.9 fusion.26
  29.6 0.7 convert_element_type.105
  30.3 0.7 add_reduce_fusion
  31.0 0.1 copy.40
  31.1 2.1 %sort.17 = (s32[64]{0:T(128)}, s32[64]{0:T(128)S(1)}) sort(s32[64]{0:T(128)S(1)} %subtract_bitcast_fusion, s32[64]{0:T(128)S(1)} %iota.88), dimensions={0}, to_apply=%region_3.4 | sort | flops 384 | bytes 1024 | tf_op jit(solution)/shard_map/jit(argsort)/sort | solution.py:119
  33.2 0.8 gather_fusion.1
  34.6 0.1 copy.39
  34.7 0.9 bitcast_multiply_fusion.1
  35.6 0.1 iota_add_fusion
  35.7 0.0 copy-done
  35.7 0.2 fusion.40
  36.0 18.0 %all-to-all-done.1 = bf16[32,2,64,128]{3,2,1,0:T(8,128)(2,1)S(1)} async-done(((bf16[32,2,64,128]{3,2,1,0:T(8,128)(2,1)}), bf16[32,2,64,128]{3,2,1,0:T(8,128)(2,1)S(1)}, u32[]{:S(2)}, u32[]{:S(2)}) %all-to-all-start.1) | async-done | bytes 1048608 | tf_op jit(solution)/shard_map/all_to_all | solution.py:106
  54.0 104.4 %conditional.1 = (bf16[64,64,128]{2,1,0:T(8,128)(2,1)S(1)}) conditional(s32[]{:T(128)} %convert_element_type.102, () %tuple.16, (f32[64,21]{0,1:T(8,128)S(1)}, bf16[21,31]{1,0:T(8,128)(2,1)}, bf16[64,64,31]{1,2,0:T(8,128)(2,1)}, bf16[32,2,64,128]{3,2,1,0:T(8,128)(2,1)S(1)}, s32[64,1]{0,1:T(1,128)S(1)}, /*index=5*/f32[128,1,128,31]{2,0,3,1:T(8,128)S(1)}, ...), branch_computations={%region_6.7_spmd, %region_7.9_spmd} | conditional | flops 4607282176 | bytes 120373048 | solution.py:69
  54.0 6.8 %multiply_reduce_fusion = bf16[128,21,128]{2,0,1:T(8,128)(2,1)} fusion(f32[21,31]{1,0:T(8,128)S(1)} %get-tuple-element.58, f32[128,128,31]{1,0,2:T(8,128)S(1)} %bitcast.66), kind=kLoop, calls=%fused_computation.5 | loop fusion | flops 20987904 | bytes 2722348 | tf_op jit(solution)/shard_map/reduce_sum | solution.py:42
  60.7 1.4 copy.30
  62.2 0.8 gather_fusion
  62.9 10.4 %convolution_convert_fusion = bf16[4096,2688]{1,0:T(8,128)(2,1)} fusion(bf16[4096,128]{1,0:T(8,128)(2,1)S(1)} %bitcast.67, bf16[128,2688]{0,1:T(8,128)(2,1)S(1)} %bitcast.69), kind=kOutput, calls=%fused_computation.6 | convolution fusion | flops 2829582336 | bytes 23756800 | tf_op jit(solution)/shard_map/while/body/eval_jaxpr/cond/branch_1_fun/dot_general | solution.py:52
  73.3 0.0 copy-start.5
  73.3 0.0 copy-start.4
  73.3 36.5 %reshape.166 = bf16[64,64,21,128]{3,2,1,0:T(8,128)(2,1)} reshape(bf16[4096,2688]{1,0:T(8,128)(2,1)} %convolution_convert_fusion) | data formatting | bytes 44040192 | tf_op jit(solution)/shard_map/while/body/eval_jaxpr/cond/branch_1_fun/reshape | solution.py:55
  109.8 0.0 copy-done.5
  109.8 0.0 copy-done.4
  109.8 10.4 %convert_bitcast_fusion = bf16[64,64,21,64]{3,0,1,2:T(8,128)(2,1)} fusion(bf16[64,64,31]{1,2,0:T(8,128)(2,1)S(1)} %copy-done.4, f32[21,31]{1,0:T(8,128)S(1)} %convert_element_type.75, f32[64,21]{0,1:T(8,128)S(1)} %get-tuple-element.52), kind=kOutput, calls=%fused_computation.10 | convolution fusion | flops 346899840 | bytes 11271980 | tf_op jit(solution)/shard_map/while/body/eval_jaxpr/cond/branch_1_fun/rat,gkt->grka/dot_general | solution.py:57
  120.2 37.8 %bitcast_convert_fusion = bf16[64,64,128]{2,1,0:T(8,128)(2,1)S(1)} fusion(bf16[64,64,21,128]{3,2,1,0:T(8,128)(2,1)} %reshape.166, bf16[64,64,21,64]{3,0,1,2:T(8,128)(2,1)} %convert_bitcast_fusion), kind=kOutput, calls=%fused_computation.11 | convolution fusion | flops 1409810432 | bytes 34078720 | tf_op jit(solution)/shard_map/while/body/eval_jaxpr/cond/branch_1_fun/grka,gakc->grc/dot_general | solution.py:60
  158.3 0.0 copy-start.2
  158.4 1.0 copy-done.2
  159.3 0.2 broadcast.116
  159.6 0.0 copy-start.6
  159.6 6.2 %scatter_fusion.1 = bf16[64,64,128]{2,1,0:T(8,128)(2,1)S(1)} fusion(bf16[64,64,128]{2,1,0:T(8,128)(2,1)S(1)} %broadcast.116, s32[64]{0:T(128)S(1)} %get-tuple-element.70, bf16[64,64,128]{2,1,0:T(8,128)(2,1)} %copy-done.2), kind=kCustom, calls=%fused_computation.4 | custom fusion | bytes 3145984 | tf_op jit(solution)/shard_map/scatter | solution.py:124
  165.8 0.0 copy-start.1
  165.8 3.6 %fusion.17 = bf16[64,64,384]{2,1,0:T(8,128)(2,1)S(1)} fusion(s32[64,128]{1,0:T(8,128)S(1)} %iota_add_fusion, bf16[64,64,128]{2,1,0:T(8,128)(2,1)S(1)} %scatter_fusion.1, f32[64]{0:T(128)S(1)} %get-tuple-element.77), kind=kOutput, calls=%fused_computation.27 | convolution fusion | flops 408944640 | bytes 4227328 | tf_op jit(solution)/shard_map/sab,sbc->sac/dot_general | solution.py:140
  169.4 4.5 %fusion.19 = f32[384,384]{1,0:T(8,128)S(1)} fusion(bf16[64,64,384]{2,1,0:T(8,128)(2,1)S(1)} %fusion.17, s32[64,64]{0,1:T(8,128)S(1)} %iota_add_fusion.1), kind=kOutput, calls=%fused_computation.31 | convolution fusion | flops 1209532416 | bytes 3751936 | tf_op jit(solution)/shard_map/rsa,sac->rc/dot_general | solution.py:146
  174.0 0.4 fusion.22
  174.3 0.0 copy-start.3
  174.3 3.2 %collective-permute-start = (f32[15,384]{1,0:T(8,128)S(1)}, f32[15,384]{1,0:T(8,128)S(1)}, u32[]{:S(2)}, u32[]{:S(2)}) collective-permute-start(f32[15,384]{1,0:T(8,128)S(1)} %get-tuple-element.73), channel_id=1, source_target_pairs={{0,8},{8,16},{16,24},{1,9},{9,17},{17,25},{2,10},{10,18},{18,26},{... | collective-permute-start | bytes 69128 | tf_op jit(solution)/shard_map/ppermute | solution.py:20
  177.6 1.3 collective-permute-start.1
  178.9 0.0 collective-permute-done
  178.9 3.2 %collective-permute-done.1 = f32[15,384]{1,0:T(8,128)S(1)} collective-permute-done((f32[15,384]{1,0:T(8,128)S(1)}, f32[15,384]{1,0:T(8,128)S(1)}, u32[]{:S(2)}, u32[]{:S(2)}) %collective-permute-start.1) | collective-permute-done | bytes 23072 | tf_op jit(solution)/shard_map/ppermute | solution.py:21
  182.2 0.1 pad_maximum_fusion.2
  182.3 4.3 %collective-permute-start.2 = (f32[414,15]{1,0:T(8,128)S(1)}, f32[414,15]{1,0:T(8,128)S(1)}, u32[]{:S(2)}, u32[]{:S(2)}) collective-permute-start(f32[414,15]{1,0:T(8,128)S(1)} %get-tuple-element.71), channel_id=1, source_target_pairs={{0,1},{1,2},{2,3},{3,4},{4,5},{5,6},{6,7},{8,9},{9,10},{10,11},{11... | collective-permute-start | bytes 74528 | tf_op jit(solution)/shard_map/ppermute | solution.py:20
  186.6 1.9 collective-permute-start.3
  188.5 0.0 copy-done.6
  188.5 2.0 %select_reduce_fusion = f32[384,414]{0,1:T(8,128)S(1)} fusion(f32[31]{0:T(128)S(1)} %copy-done.6, s32[384,414]{0,1:T(8,128)S(1)} %iota_subtract_fusion), kind=kLoop, calls=%fused_computation.18 | loop fusion | flops 14625792 | bytes 1271932 | tf_op jit(solution)/shard_map/reduce_sum | solution.py:162
  190.5 0.0 collective-permute-done.2
  190.5 3.2 %collective-permute-done.3 = f32[414,15]{1,0:T(8,128)S(1)} collective-permute-done((f32[414,15]{1,0:T(8,128)S(1)}, f32[414,15]{1,0:T(8,128)S(1)}, u32[]{:S(2)}, u32[]{:S(2)}) %collective-permute-start.3) | collective-permute-done | bytes 24872 | tf_op jit(solution)/shard_map/ppermute | solution.py:21
  193.7 2.3 %fusion.27 = f32[384,414]{0,1:T(8,128)S(1)} fusion(f32[384,414]{0,1:T(8,128)S(1)} %select_reduce_fusion, f32[414,15]{1,0:T(8,128)S(1)} %collective-permute-done.3, f32[15,384]{1,0:T(8,128)S(1)} %collective-permute-done.1, f32[384,384]{1,0:T(8,128)S(1)} %fusion.22, f32[15,384]{1,0:T(8,128)S(1)} %collective-permute-done, f32[414,15]{1,0:T(8,128)S(1)} %collective-permute-done.2), kind=kOutput, calls=%fused_computation.40 | convolution fusion | flops 790478336 | bytes 1957392 | tf_op jit(solution)/shard_map/dot_general | solution.py:163
  196.1 2.4 %fusion.57 = f32[384,384]{1,0:T(8,128)} fusion(f32[384,414]{0,1:T(8,128)S(1)} %fusion.27, f32[384,414]{0,1:T(8,128)S(1)} %select_reduce_fusion), kind=kOutput, calls=%fused_computation.99 | convolution fusion | flops 732561408 | bytes 1861632 | tf_op jit(solution)/shard_map/dot_general | solution.py:164
  198.4 0.0 copy-done.3
  198.4 0.0 copy-done.1
  (13 shorter events, 0.1 us)
Async XLA Ops:
  0.6 35.1 %copy-start = (f32[256,21]{0,1:T(8,128)S(1)}, f32[256,21]{0,1:T(8,128)}, u32[]{:S(2)}) copy-start(f32[256,21]{0,1:T(8,128)} %param.19) | copy-start | bytes 64516
  5.1 17.7 %all-to-all-start = ((s32[32,2,4]{2,1,0:T(2,128)}), s32[32,2,4]{2,1,0:T(2,128)S(1)}, u32[]{:S(2)}, u32[]{:S(2)}) async-start(s32[32,2,4]{2,1,0:T(2,128)} %bitcast.17), calls=%async_computation | async-start | bytes 65536 | tf_op jit(solution)/shard_map/all_to_all | solution.py:113
  22.8 31.2 %all-to-all-start.1 = ((bf16[32,2,64,128]{3,2,1,0:T(8,128)(2,1)}), bf16[32,2,64,128]{3,2,1,0:T(8,128)(2,1)S(1)}, u32[]{:S(2)}, u32[]{:S(2)}) async-start(bf16[32,2,64,128]{3,2,1,0:T(8,128)(2,1)} %bitcast.26), calls=%async_computation.1 | async-start | bytes 2097152 | tf_op jit(solution)/shard_map/all_to_all | solution.py:106
  73.3 36.5 %copy-start.5 = (bf16[21,31]{1,0:T(8,128)(2,1)S(1)}, bf16[21,31]{1,0:T(8,128)(2,1)}, u32[]{:S(2)}) copy-start(bf16[21,31]{1,0:T(8,128)(2,1)} %get-tuple-element.64) | copy-start | bytes 3910 | tf_op jit(solution)/shard_map/while/body/eval_jaxpr/cond
  73.3 36.5 %copy-start.4 = (bf16[64,64,31]{1,2,0:T(8,128)(2,1)S(1)}, bf16[64,64,31]{1,2,0:T(8,128)(2,1)}, u32[]{:S(2)}) copy-start(bf16[64,64,31]{1,2,0:T(8,128)(2,1)} %get-tuple-element.54) | copy-start | bytes 761860 | tf_op jit(solution)/shard_map/while/body/eval_jaxpr/cond
  158.3 1.0 copy-start.2
  159.6 28.9 %copy-start.6 = (f32[31]{0:T(128)S(1)}, f32[31]{0:T(128)}, u32[]{:S(2)}) copy-start(f32[31]{0:T(128)} %param.21) | copy-start | bytes 376
  165.8 32.6 %copy-start.1 = (f32[256,21]{0,1:T(8,128)S(1)}, f32[256,21]{0,1:T(8,128)}, u32[]{:S(2)}) copy-start(f32[256,21]{0,1:T(8,128)} %param.19) | copy-start | bytes 64516
  174.3 24.1 %copy-start.3 = (f32[384,384]{1,0:T(8,128)}, f32[384,384]{1,0:T(8,128)S(1)}, u32[]{:S(2)}) copy-start(f32[384,384]{1,0:T(8,128)S(1)} %fusion.22) | copy-start | bytes 1769476
  174.3 4.6 %collective-permute-start = (f32[15,384]{1,0:T(8,128)S(1)}, f32[15,384]{1,0:T(8,128)S(1)}, u32[]{:S(2)}, u32[]{:S(2)}) collective-permute-start(f32[15,384]{1,0:T(8,128)S(1)} %get-tuple-element.73), channel_id=1, source_target_pairs={{0,8},{8,16},{16,24},{1,9},{9,17},{17,25},{2,10},{10,18},{18,26},{... | collective-permute-start | bytes 69128 | tf_op jit(solution)/shard_map/ppermute | solution.py:20
  177.6 4.6 %collective-permute-start.1 = (f32[15,384]{1,0:T(8,128)S(1)}, f32[15,384]{1,0:T(8,128)S(1)}, u32[]{:S(2)}, u32[]{:S(2)}) collective-permute-start(f32[15,384]{1,0:T(8,128)S(1)} %get-tuple-element.74), channel_id=1, source_target_pairs={{8,0},{16,8},{24,16},{9,1},{17,9},{25,17},{10,2},{18,10},{26,18},{... | collective-permute-start | bytes 69128 | tf_op jit(solution)/shard_map/ppermute | solution.py:21
  182.3 8.2 %collective-permute-start.2 = (f32[414,15]{1,0:T(8,128)S(1)}, f32[414,15]{1,0:T(8,128)S(1)}, u32[]{:S(2)}, u32[]{:S(2)}) collective-permute-start(f32[414,15]{1,0:T(8,128)S(1)} %get-tuple-element.71), channel_id=1, source_target_pairs={{0,1},{1,2},{2,3},{3,4},{4,5},{5,6},{6,7},{8,9},{9,10},{10,11},{11... | collective-permute-start | bytes 74528 | tf_op jit(solution)/shard_map/ppermute | solution.py:20
  186.6 7.2 %collective-permute-start.3 = (f32[414,15]{1,0:T(8,128)S(1)}, f32[414,15]{1,0:T(8,128)S(1)}, u32[]{:S(2)}, u32[]{:S(2)}) collective-permute-start(f32[414,15]{1,0:T(8,128)S(1)} %get-tuple-element.72), channel_id=1, source_target_pairs={{1,0},{2,1},{3,2},{4,3},{5,4},{6,5},{7,6},{9,8},{10,9},{11,10},{12... | collective-permute-start | bytes 74528 | tf_op jit(solution)/shard_map/ppermute | solution.py:21
where the time goes:
time: 200 us; the launch traced here: 198 us
  matrix products  72.9 us (36%)
  local copies, waits for them, and re-layouts  58.8 us (29%)
  waiting for transfers between devices  24.4 us (12%)
  starting transfers between devices  23.7 us (12%)
  other arithmetic  16.8 us (8%)
    dot_general x1, matrix products, compute(): jnp.einsum('grka,gakc->grc', row_table, section, preferred_element_type=j...  37.8 us
    reshape x1, local copies, waits for them, and re-layouts, compute(): section = section.astype(jnp.bfloat16).reshape(group, rows, kinds, cols)  36.5 us
    all_to_all x1, waiting for transfers between devices, shards(): lax.all_to_all(outgoing.reshape(owners, CAP, rows, cols), ('prow', 'pcol'...  18 us
    dot_general x1, matrix products, compute(): jnp.einsum('rat,gkt->grka', row_hits, scaled, preferred_element_type=jnp....  10.4 us
    dot_general x1, matrix products, compute(): jnp.dot(piece.reshape(group * rows, cols), col_table, preferred_element_t...  10.4 us
    scatter x1, local copies, waits for them, and re-layouts, shards(): jnp.zeros((owners * CAP, rows, cols), jnp.bfloat16).at[slot].set(blocks)  9.08 us
    ppermute x2, starting transfers between devices, padded_2(): before = lax.ppermute(last, axis, up)  7.52 us
    all_to_all x1, starting transfers between devices, shards(): lax.all_to_all(info_out.reshape(owners, CAP, 4), ('prow', 'pcol'), split_...  7.1 us
  transfers between devices with their start and end apart: 6, of which 3 were waited for; matrix products, arithmetic and copies ran while one was open for 10% of the time, Pallas kernels for 0%

commit v1 on v0

v1 whole, which is shorter than its diff:
```python
import functools

import jax
import jax.numpy as jnp
from jax import lax
from jax.experimental import pallas as pl
from jax.experimental.pallas import tpu as pltpu
from jax.sharding import PartitionSpec as P

DET_R = 15
PATCH = 384
CAP = 2
LANES = 128
MESH = pl.DeviceIdType.MESH
EXACT = lax.Precision.HIGHEST


def padded_2(value, sides, width):
    for axis, dim in sides:
        size, length = (lax.axis_size(axis), value.shape[dim])
        up = [(i, (i + 1) % size) for i in range(size - 1)]
        down = [(j, i) for i, j in up]
        last = lax.slice_in_dim(value, length - width, length, axis=dim)
        leading = lax.slice_in_dim(value, 0, width, axis=dim)
        before = lax.ppermute(last, axis, up)
        after = lax.ppermute(leading, axis, down)
        value = jnp.concatenate([before, value, after], axis=dim)
    return value


def tables_kernel(
    kinds,
    slots,
    owner_col,
    owner_row,
    feats,
    exposure_col,
    table,
    col_src,
    row_src,
    info_out,
    coef_out,
    col_out,
    row_out,
):
    count = owner_col.shape[0]
    entries = table.shape[0]
    at_sub = lax.broadcasted_iota(jnp.int32, (count, count), 0)
    at_lane = lax.broadcasted_iota(jnp.int32, (count, count), 1)
    same = (owner_col[...] == owner_row[...]) & (at_sub < at_lane)
    rank = jnp.sum(same.astype(jnp.int32), axis=0, keepdims=True)
    slot = owner_row[...] * CAP + rank
    pick = (lax.broadcasted_iota(jnp.int32, (slots, count), 0) == slot).astype(jnp.float32)
    hits = (
        exposure_col[...] == lax.broadcasted_iota(jnp.int32, (count, entries), 1)
    ).astype(jnp.float32)
    found = jnp.dot(hits, table[...], precision=EXACT, preferred_element_type=jnp.float32)
    lane = lax.broadcasted_iota(jnp.int32, (count, LANES), 1)
    rounded = found.astype(jnp.bfloat16).astype(jnp.float32)
    found = jnp.where(lane == kinds, rounded, found)
    merged = jnp.where(lane <= kinds, found, feats[...])
    info = jnp.dot(pick, merged, precision=EXACT, preferred_element_type=jnp.float32)
    info_out[...] = info
    width = coef_out.shape[1]
    half = width // (kinds + 1)
    spread = (
        lax.broadcasted_iota(jnp.int32, (LANES, width), 0)
        == lax.broadcasted_iota(jnp.int32, (LANES, width), 1) // half
    ).astype(jnp.float32)
    coef_out[...] = jnp.dot(info, spread, precision=EXACT, preferred_element_type=jnp.float32)
    cols = col_out.shape[0]
    down = lax.broadcasted_iota(jnp.int32, (cols, LANES), 0)
    over = lax.broadcasted_iota(jnp.int32, (cols, LANES), 1)
    near = jnp.abs(over - down) <= DET_R
    for k in range(kinds):
        source = jnp.broadcast_to(col_src[k : k + 1, :], (cols, LANES))
        rolled = pltpu.roll(source, 0, 1, stride=1, stride_axis=0)
        col_out[:, k * LANES : (k + 1) * LANES] = jnp.where(near, rolled, 0.0).astype(jnp.bfloat16)
    rows = row_out.shape[0]
    down = lax.broadcasted_iota(jnp.int32, (rows, LANES), 0)
    over = lax.broadcasted_iota(jnp.int32, (rows, LANES), 1) % rows
    near = jnp.abs(over - down) <= DET_R
    for k in range(row_src.shape[0]):
        source = jnp.broadcast_to(row_src[k : k + 1, :], (rows, LANES))
        rolled = pltpu.roll(source, 0, 1, stride=1, stride_axis=0)
        row_out[:, k * LANES : (k + 1) * LANES] = jnp.where(near, rolled, 0.0)


def route_kernel(
    owners,
    ncol,
    kinds,
    picks,
    blocks,
    coefs,
    info,
    col_table,
    row_table,
    pixels_out,
    info_out,
    outgoing,
    sems,
):
    me = lax.axis_index("prow") * ncol + lax.axis_index("pcol")
    rows, cols = blocks.shape[1:]
    barrier = pltpu.get_barrier_semaphore()

    def place(device):
        return (device // ncol, device % ncol)

    def greet(i, carry):
        other = lax.rem(me + i, owners)
        pl.semaphore_signal(barrier, inc=1, device_id=place(other), device_id_type=MESH)
        return carry

    lax.fori_loop(1, owners, greet, 0)
    pl.semaphore_wait(barrier, owners - 1)

    def tell(i, carry):
        other = lax.rem(me + i, owners)
        pltpu.make_async_remote_copy(
            src_ref=info.at[other],
            dst_ref=info_out.at[me],
            send_sem=sems.at[0],
            recv_sem=sems.at[1],
            device_id=place(other),
            device_id_type=MESH,
        ).start()
        return carry

    lax.fori_loop(1, owners, tell, 0)
    info_out[me] = info[me]

    def matched_pair(other):
        first = other * CAP
        pair = jnp.concatenate([blocks[picks[first + j]] for j in range(CAP)], axis=0)
        coefs_of = [coefs[pl.ds(first + j, 1), :] for j in range(CAP)]
        totals = [jnp.zeros((rows, cols), jnp.float32) for _ in range(CAP)]
        step = 4
        for k in range(0, kinds, step):
            more = min(step, kinds - k)
            section = jnp.dot(
                pair,
                col_table[:, k * cols : (k + more) * cols],
                preferred_element_type=jnp.float32,
            ).astype(jnp.bfloat16)
            base = row_table[:, k * rows : (k + more) * rows]
            for j in range(CAP):
                stacked = jnp.concatenate(
                    [
                        section[j * rows : (j + 1) * rows, m * cols : (m + 1) * cols]
                        for m in range(more)
                    ],
                    axis=0,
                )
                coef = coefs_of[j][:, k * rows : (k + more) * rows]
                scaled = (coef * base).astype(jnp.bfloat16)
                totals[j] = totals[j] + jnp.dot(
                    scaled, stacked, preferred_element_type=jnp.float32
                )
        done = []
        for j in range(CAP):
            weight = coefs_of[j][:, kinds * rows : kinds * rows + 1]
            matched = totals[j].astype(jnp.bfloat16).astype(jnp.float32)
            done.append((weight * matched).astype(jnp.bfloat16))
        return jnp.concatenate(done, axis=0)

    def send(i, carry):
        other = lax.rem(me + i, owners)
        outgoing[other] = matched_pair(other)
        pltpu.make_async_remote_copy(
            src_ref=outgoing.at[other],
            dst_ref=pixels_out.at[me],
            send_sem=sems.at[2],
            recv_sem=sems.at[3],
            device_id=place(other),
            device_id_type=MESH,
        ).start()
        return carry

    lax.fori_loop(1, owners, send, 0)
    pixels_out[me] = matched_pair(me)
    others = pl.ds(0, owners - 1)
    for ref, pair in ((info, 0), (outgoing, 2)):
        for which in range(2):
            pltpu.make_async_copy(ref.at[others], ref.at[others], sems.at[pair + which]).wait()


def place_kernel(slots, rows, span_rows, span_cols, pixels, info, coadd, total):
    total[...] = jnp.zeros_like(total)
    cols = pixels.shape[2]
    lane = lax.broadcasted_iota(jnp.int32, (rows, cols), 1)

    def add(s, carry):
        row = span_rows[s]
        col = span_cols[s]
        tile = col // cols
        shift = col - tile * cols
        block = pltpu.roll(pixels[s].astype(jnp.float32), shift, 1)
        here = pl.ds(row, rows)
        left = lane >= shift
        total[tile, here, :] += jnp.where(left, block, 0.0)
        total[tile + 1, here, :] += jnp.where(left, 0.0, block)
        return carry

    lax.fori_loop(0, slots, add, 0)
    weight, top, left = info[:, 0:1], info[:, 1:2], info[:, 2:3]
    span = lax.broadcasted_iota(jnp.int32, (slots, PATCH), 1).astype(jnp.float32)
    row_weight = jnp.where((span >= top) & (span < top + rows), weight, 0.0).astype(jnp.bfloat16)
    col_cover = jnp.where((span >= left) & (span < left + cols), 1.0, 0.0).astype(jnp.bfloat16)
    depth = lax.dot_general(
        row_weight, col_cover, (((0,), (0,)), ((), ())), preferred_element_type=jnp.float32
    )
    value = jnp.concatenate([total[t] for t in range(PATCH // cols)], axis=1)
    coadd[...] = value / jnp.maximum(depth, 1.0)


def detect(coadd, det_taps):
    span = jnp.arange(PATCH)
    padded = padded_2(coadd, (("prow", 0), ("pcol", 1)), DET_R)
    wide = jnp.arange(PATCH + 2 * DET_R)
    reach = jnp.arange(2 * DET_R + 1)
    band_hits = (wide[None, :, None] - span[:, None, None] == reach[None, None, :]).astype(
        jnp.float32
    )
    band = jnp.sum(band_hits * det_taps[None, None, :], axis=2)
    across = jnp.dot(band, padded, precision=EXACT)
    return jnp.dot(across, band.T, precision=EXACT)


def shards(
    blocks,
    owner,
    row_offset,
    col_offset,
    exposure,
    basis_rows,
    basis_cols,
    coef_table,
    weight_table,
    det_taps,
):
    ncol = lax.axis_size("pcol")
    owners = lax.axis_size("prow") * ncol
    count, rows, cols = blocks.shape
    kinds, taps = basis_rows.shape
    entries = coef_table.shape[0]
    slots = owners * CAP
    vmem = pl.BlockSpec(memory_space=pltpu.VMEM)
    smem = pl.BlockSpec(memory_space=pltpu.SMEM)
    half = taps // 2

    feats = jnp.stack([row_offset, col_offset, jnp.arange(count, dtype=jnp.int32)], axis=1)
    feats = jnp.pad(feats.astype(jnp.float32), ((0, 0), (kinds + 1, LANES - kinds - 4)))
    table = jnp.concatenate([coef_table, weight_table[:, None]], axis=1)
    table = jnp.pad(table, ((0, 0), (0, LANES - kinds - 1)))
    flipped = jnp.pad(basis_cols.astype(jnp.float32)[:, ::-1], ((0, 0), (0, LANES - taps)))
    col_src = jnp.roll(flipped, -half, axis=1)
    narrow = jnp.pad(basis_rows.astype(jnp.float32), ((0, kinds % 2), (0, rows - taps)))
    row_src = jnp.roll(narrow.reshape(-1, 2 * rows), -half, axis=1)
    pairs = row_src.shape[0]

    info, coefs, col_table, row_table = pl.pallas_call(
        functools.partial(tables_kernel, kinds, slots),
        out_shape=(
            jax.ShapeDtypeStruct((slots, LANES), jnp.float32),
            jax.ShapeDtypeStruct((slots, (kinds + 1) * rows), jnp.float32),
            jax.ShapeDtypeStruct((cols, kinds * cols), jnp.bfloat16),
            jax.ShapeDtypeStruct((rows, pairs * 2 * rows), jnp.float32),
        ),
        in_specs=[vmem] * 7,
        out_specs=(vmem,) * 4,
        name="tables",
    )(owner, owner.reshape(1, count), feats, exposure[:, None], table, col_src, row_src)

    picks = info[:, kinds + 3].astype(jnp.int32)
    told = info[:, kinds : kinds + 3].reshape(owners, 1, CAP * 3)
    told = jnp.pad(told, ((0, 0), (0, 0), (0, LANES - CAP * 3)))
    pixels, heard = pl.pallas_call(
        functools.partial(route_kernel, owners, ncol, kinds),
        out_shape=(
            jax.ShapeDtypeStruct((owners, CAP * rows, cols), jnp.bfloat16),
            jax.ShapeDtypeStruct((owners, 1, LANES), jnp.float32),
        ),
        in_specs=[smem] + [vmem] * 5,
        out_specs=(vmem, vmem),
        scratch_shapes=[
            pltpu.VMEM((owners, CAP * rows, cols), jnp.bfloat16),
            pltpu.SemaphoreType.DMA((4,)),
        ],
        compiler_params=pltpu.CompilerParams(
            collective_id=0, has_side_effects=True, vmem_limit_bytes=48 * 1024 * 1024
        ),
        name="route",
    )(picks, blocks, coefs, told, col_table, row_table)

    told = heard[:, 0, : CAP * 3].reshape(slots, 3)
    spans = told[:, 1:].astype(jnp.int32)
    coadd = pl.pallas_call(
        functools.partial(place_kernel, slots, rows),
        out_shape=jax.ShapeDtypeStruct((PATCH, PATCH), jnp.float32),
        in_specs=[smem, smem, vmem, vmem],
        out_specs=vmem,
        scratch_shapes=[pltpu.VMEM((PATCH // cols + 1, PATCH, cols), jnp.float32)],
        compiler_params=pltpu.CompilerParams(vmem_limit_bytes=48 * 1024 * 1024),
        name="place",
    )(spans[:, 0], spans[:, 1], pixels.reshape(slots, rows, cols), told)
    return (coadd, detect(coadd, det_taps))


def solution(mesh):
    in_specs = (
        P(("prow", "pcol"), None, None),
        P(("prow", "pcol"), None),
        P(("prow", "pcol")),
        P(("prow", "pcol")),
        P(("prow", "pcol")),
        P(),
        P(),
        P(),
        P(),
        P(),
    )
    out_specs = (P("prow", "pcol"), P("prow", "pcol"))
    return jax.shard_map(shards, mesh=mesh, in_specs=in_specs, out_specs=out_specs, check_vma=False)
```

time: 200 us -> 91.1 us (0.46)
  matrix products: 72.9 us -> 4.66 us
  Pallas kernels: 0 us -> 51 us
  local copies, waits for them, and re-layouts: 58.8 us -> 11.3 us
  waiting for transfers between devices: 24.4 us -> 6.42 us
  starting transfers between devices: 23.7 us -> 9.63 us
  other arithmetic: 16.8 us -> 6.67 us
    dot_general x10 -> x2, matrix products: 72.9 us -> 4.66 us  [the longest x1 2.35 us: detect(): return jnp.dot(across, band.T, precision=EXACT)]
    pallas_call x0 -> x3, Pallas kernels: none -> 51 us  [the longest x1 41.3 us: shards(): pl.pallas_call(functools.partial(route_kernel, owners, ncol, kinds), out_...]
    reshape x1 -> x2, local copies, waits for them, and re-layouts: 36.5 us -> 0.15 us  [the longest x1 0.07 us: shards(): told = info[:, kinds:kinds + 3].reshape(owners, 1, CAP * 3)]
    all_to_all x2 -> x0, waiting for transfers between devices: 18 us -> none  [the longest x1 18 us: shards(): lax.all_to_all(outgoing.reshape(owners, CAP, rows, cols), ('prow', 'pcol'...]
    scatter x3 -> x0, local copies, waits for them, and re-layouts: 16.6 us -> none  [the longest x1 9.08 us: shards(): jnp.zeros((owners * CAP, rows, cols), jnp.bfloat16).at[slot].set(blocks)]
    all_to_all x2 -> x0, starting transfers between devices: 12.9 us -> none  [the longest x1 7.1 us: shards(): lax.all_to_all(info_out.reshape(owners, CAP, 4), ('prow', 'pcol'), split_...]
    reduce_sum x3 -> x1, other arithmetic: 9.59 us -> 2 us  [detect(): band = jnp.sum(band_hits * det_taps[None, None, :], axis=2)]
    unnamed x12 -> x13, local copies, waits for them, and re-layouts: 1.15 us -> 4.43 us
  transfers between devices with their start and end apart: 6 -> 4, of which waited for: 3 -> 2; matrix products, arithmetic and copies ran while one was open for 10% -> 2% of each run, Pallas kernels for 0% -> 0%
where the time goes in v1:
time: 91.1 us; the launch traced here: 90.5 us
  Pallas kernels  51 us (56%)
  local copies, waits for them, and re-layouts  11.3 us (12%)
  starting transfers between devices  9.63 us (11%)
  other arithmetic  6.67 us (7%)
  waiting for transfers between devices  6.42 us (7%)
  matrix products  4.66 us (5%)
    pallas_call x1, Pallas kernels, shards(): pl.pallas_call(functools.partial(route_kernel, owners, ncol, kinds), out_...  41.3 us
    pallas_call x1, Pallas kernels, shards(): pl.pallas_call(functools.partial(place_kernel, slots, rows), out_shape=ja...  6.77 us
    ppermute x2, waiting for transfers between devices, padded_2(): after = lax.ppermute(leading, axis, down)  6.42 us
    ppermute x2, starting transfers between devices, padded_2(): before = lax.ppermute(last, axis, up)  6.42 us
    unnamed x13, local copies, waits for them, and re-layouts  4.43 us
    ppermute x2, starting transfers between devices, padded_2(): after = lax.ppermute(leading, axis, down)  3.21 us
    pallas_call x1, Pallas kernels, shards(): pl.pallas_call(functools.partial(tables_kernel, kinds, slots), out_shape=...  2.94 us
    dot_general x1, matrix products, detect(): return jnp.dot(across, band.T, precision=EXACT)  2.35 us
  transfers between devices with their start and end apart: 4, of which 2 were waited for; matrix products, arithmetic and copies ran while one was open for 2% of the time, Pallas kernels for 0%

profile of v1, /device:TPU:1, one launch (start us, length us, event | category | flops | bytes accessed | tf_op | source)
XLA Modules:
  0.0 90.5 jit_solution(5955876813748089991)
XLA Ops:
  0.6 0.0 copy-start
  0.6 0.9 rev.3
  1.5 0.8 slice.65
  2.3 0.7 pad_convert_fusion
  3.0 0.1 reshape.42
  3.0 0.1 slice.66
  3.1 0.8 pad_maximum_fusion.3
  3.9 0.1 copy.35
  4.0 0.7 add_convert_fusion
  4.7 0.1 copy.34
  4.8 0.7 pad.22.table
  5.4 0.7 pad.21.feats
  6.1 0.1 pad_slice_fusion
  6.2 0.1 slice.52
  6.3 1.4 %copy.36.owner_col = s32[64,1]{1,0:T(8,128)} copy(s32[64,1]{0,1:T(1,128)} %param.11) | data formatting | bytes 512 | tf_op args[1]
  7.6 1.4 %copy.37.exposure_col = s32[64,1]{1,0:T(8,128)} copy(s32[64,1]{0,1:T(1,128)} %bitcast.16) | data formatting | bytes 512 | tf_op jit(solution)/shard_map/broadcast_in_dim | solution.py:274
  9.0 0.7 pad_maximum_fusion.5.row_src
  9.6 0.7 pad_maximum_fusion.4.col_src
  10.3 2.9 %tables.1 = (f32[64,128]{1,0:T(8,128)}, f32[64,1408]{1,0:T(8,128)}, bf16[128,2688]{1,0:T(8,128)(2,1)}, f32[64,1408]{1,0:T(8,128)}) custom-call(s32[64,1]{1,0:T(8,128)} %copy.36.owner_col, s32[1,64]{1,0:T(1,128)} %bitcast.14, f32[64,128]{1,0:T(8,128)} %pad.21.feats, s32[64,1]{1,0:T(8,128)} %copy.37.exposure_col, f32[256,128]{1,0:T(8,128)} %pad.22.table, ...), custom_call_target="tpu_custom_call" | custom-call | tf_op jit(solution)/shard_map/tables/pallas_call | solution.py:263
  13.3 0.8 slice.56
  14.1 0.9 %convert_reduce_fusion.picks = s32[64]{0:T(128)S(1)} fusion(f32[64,128]{1,0:T(8,128)} %get-tuple-element.8), kind=kLoop, calls=%fused_computation.19 | loop fusion | flops 64 | bytes 512 | tf_op jit(solution)/shard_map/convert_element_type | solution.py:276
  15.0 0.1 reshape.39
  15.1 0.0 copy-done
  15.1 0.0 copy-start.1
  15.2 1.1 %copy-done.1 = bf16[128,2688]{1,0:T(8,128)(2,1)S(1)} copy-done((bf16[128,2688]{1,0:T(8,128)(2,1)S(1)}, bf16[128,2688]{1,0:T(8,128)(2,1)}, u32[]{:S(2)}) %copy-start.1) | copy-done | bytes 688152
  16.2 0.0 copy-start.2
  16.2 1.0 %copy-done.2 = f32[64,1408]{1,0:T(8,128)S(1)} copy-done((f32[64,1408]{1,0:T(8,128)S(1)}, f32[64,1408]{1,0:T(8,128)}, u32[]{:S(2)}) %copy-start.2) | copy-done | bytes 360472
  17.2 0.0 copy-start.3
  17.2 1.0 %copy-done.3 = f32[64,1408]{1,0:T(8,128)S(1)} copy-done((f32[64,1408]{1,0:T(8,128)S(1)}, f32[64,1408]{1,0:T(8,128)}, u32[]{:S(2)}) %copy-start.3) | copy-done | bytes 360472
  18.2 41.3 %route.1 = (bf16[32,128,128]{2,1,0:T(8,128)(2,1)S(1)}, f32[32,1,128]{2,1,0:T(1,128)S(1)}) custom-call(s32[64]{0:T(128)S(1)} %convert_reduce_fusion.picks, bf16[64,64,128]{2,1,0:T(8,128)(2,1)S(1)} %copy-done, f32[64,1408]{1,0:T(8,128)S(1)} %copy-done.2, f32[32,1,128]{2,1,0:T(1,128)S(1)} %pad.25.info, bf16[128,2688]{1,0:T(8,128)(2,1)S(1)} %copy-done.1, ...), custom_call_target="tpu_custom_call" | custom-call | tf_op jit(solution)/shard_map/route/pallas_call | solution.py:279
  59.6 0.1 reshape_squeeze.3.info
  59.6 0.1 slice_convert_fusion
  59.7 0.2 slice_reduce_fusion
  59.9 6.8 %place.1 = f32[384,384]{1,0:T(8,128)} custom-call(s32[64]{0:T(128)S(1)} %get-tuple-element.15.span_rows, s32[64]{0:T(128)S(1)} %get-tuple-element.14.span_cols, bf16[64,64,128]{2,1,0:T(8,128)(2,1)S(1)} %bitcast.11, f32[64,3]{1,0:T(8,128)S(1)} %reshape_squeeze.3.info), custom_call_target="tpu_custom_call" | custom-call | tf_op jit(solution)/shard_map/place/pallas_call | solution.py:299
  66.7 0.0 copy-start.4
  66.7 0.0 copy-start.5
  66.7 0.8 fusion.11
  67.5 2.3 %collective-permute-start = (f32[15,384]{1,0:T(8,128)S(1)}, f32[15,384]{1,0:T(8,128)S(1)}, u32[]{:S(2)}, u32[]{:S(2)}) collective-permute-start(f32[15,384]{1,0:T(8,128)S(1)} %get-tuple-element.18), channel_id=1, source_target_pairs={{0,8},{8,16},{16,24},{1,9},{9,17},{17,25},{2,10},{10,18},{18,26},{... | collective-permute-start | bytes 69128 | tf_op jit(solution)/shard_map/ppermute | solution.py:25
  69.8 1.3 %collective-permute-start.1 = (f32[15,384]{1,0:T(8,128)S(1)}, f32[15,384]{1,0:T(8,128)S(1)}, u32[]{:S(2)}, u32[]{:S(2)}) collective-permute-start(f32[15,384]{1,0:T(8,128)S(1)} %get-tuple-element.19), channel_id=1, source_target_pairs={{8,0},{16,8},{24,16},{9,1},{17,9},{25,17},{10,2},{18,10},{26,18},{... | collective-permute-start | bytes 69128 | tf_op jit(solution)/shard_map/ppermute | solution.py:26
  71.2 0.0 collective-permute-done
  71.2 3.2 %collective-permute-done.1 = f32[15,384]{1,0:T(8,128)S(1)} collective-permute-done((f32[15,384]{1,0:T(8,128)S(1)}, f32[15,384]{1,0:T(8,128)S(1)}, u32[]{:S(2)}, u32[]{:S(2)}) %collective-permute-start.1) | collective-permute-done | bytes 23072 | tf_op jit(solution)/shard_map/ppermute | solution.py:26
  74.4 0.0 copy-done.4
  74.4 0.1 pad_maximum_fusion.2
  74.5 4.1 %collective-permute-start.2 = (f32[414,15]{1,0:T(8,128)S(1)}, f32[414,15]{1,0:T(8,128)S(1)}, u32[]{:S(2)}, u32[]{:S(2)}) collective-permute-start(f32[414,15]{1,0:T(8,128)S(1)} %get-tuple-element.16), channel_id=1, source_target_pairs={{0,1},{1,2},{2,3},{3,4},{4,5},{5,6},{6,7},{8,9},{9,10},{10,11},{11... | collective-permute-start | bytes 74528 | tf_op jit(solution)/shard_map/ppermute | solution.py:25
  78.6 1.9 %collective-permute-start.3 = (f32[414,15]{1,0:T(8,128)S(1)}, f32[414,15]{1,0:T(8,128)S(1)}, u32[]{:S(2)}, u32[]{:S(2)}) collective-permute-start(f32[414,15]{1,0:T(8,128)S(1)} %get-tuple-element.17), channel_id=1, source_target_pairs={{1,0},{2,1},{3,2},{4,3},{5,4},{6,5},{7,6},{9,8},{10,9},{11,10},{12... | collective-permute-start | bytes 74528 | tf_op jit(solution)/shard_map/ppermute | solution.py:26
  80.6 0.0 copy-done.5
  80.6 2.0 %select_reduce_fusion = f32[384,414]{0,1:T(8,128)S(1)} fusion(f32[31]{0:T(128)S(1)} %copy-done.5, s32[384,414]{0,1:T(8,128)S(1)} %iota_subtract_fusion), kind=kLoop, calls=%fused_computation | loop fusion | flops 14625792 | bytes 1271932 | tf_op jit(solution)/shard_map/reduce_sum | solution.py:226
  82.6 0.0 collective-permute-done.2
  82.6 3.2 %collective-permute-done.3 = f32[414,15]{1,0:T(8,128)S(1)} collective-permute-done((f32[414,15]{1,0:T(8,128)S(1)}, f32[414,15]{1,0:T(8,128)S(1)}, u32[]{:S(2)}, u32[]{:S(2)}) %collective-permute-start.3) | collective-permute-done | bytes 24872 | tf_op jit(solution)/shard_map/ppermute | solution.py:26
  85.8 2.3 %fusion = f32[384,414]{0,1:T(8,128)S(1)} fusion(f32[384,414]{0,1:T(8,128)S(1)} %select_reduce_fusion, f32[414,15]{1,0:T(8,128)S(1)} %collective-permute-done.3, f32[15,384]{1,0:T(8,128)S(1)} %collective-permute-done.1, f32[384,384]{1,0:T(8,128)S(1)} %copy-done.4, f32[15,384]{1,0:T(8,128)S(1)} %collective-permute-done, f32[414,15]{1,0:T(8,128)S(1)} %collective-permute-done.2), kind=kOutput, calls=%fused_computation.2 | convolution fusion | flops 790478336 | bytes 1957392 | tf_op jit(solution)/shard_map/dot_general | solution.py:227
  88.1 2.4 %fusion.12 = f32[384,384]{1,0:T(8,128)} fusion(f32[384,414]{0,1:T(8,128)S(1)} %fusion, f32[384,414]{0,1:T(8,128)S(1)} %select_reduce_fusion), kind=kOutput, calls=%fused_computation.29 | convolution fusion | flops 732561408 | bytes 1861632 | tf_op jit(solution)/shard_map/dot_general | solution.py:228
  (4 shorter events, 0.1 us)
Async XLA Ops:
  0.6 14.5 %copy-start = (bf16[64,64,128]{2,1,0:T(8,128)(2,1)S(1)}, bf16[64,64,128]{2,1,0:T(8,128)(2,1)}, u32[]{:S(2)}) copy-start(bf16[64,64,128]{2,1,0:T(8,128)(2,1)} %blocks.1) | copy-start | bytes 3145732
  15.1 1.1 %copy-start.1 = (bf16[128,2688]{1,0:T(8,128)(2,1)S(1)}, bf16[128,2688]{1,0:T(8,128)(2,1)}, u32[]{:S(2)}) copy-start(bf16[128,2688]{1,0:T(8,128)(2,1)} %get-tuple-element.10.col_table) | copy-start | bytes 2064388
  16.2 1.0 %copy-start.2 = (f32[64,1408]{1,0:T(8,128)S(1)}, f32[64,1408]{1,0:T(8,128)}, u32[]{:S(2)}) copy-start(f32[64,1408]{1,0:T(8,128)} %get-tuple-element.9.coefs) | copy-start | bytes 1081348
  17.2 1.0 %copy-start.3 = (f32[64,1408]{1,0:T(8,128)S(1)}, f32[64,1408]{1,0:T(8,128)}, u32[]{:S(2)}) copy-start(f32[64,1408]{1,0:T(8,128)} %get-tuple-element.11.row_table) | copy-start | bytes 1081348
  66.7 7.7 %copy-start.4 = (f32[384,384]{1,0:T(8,128)S(1)}, f32[384,384]{1,0:T(8,128)}, u32[]{:S(2)}) copy-start(f32[384,384]{1,0:T(8,128)} %place.1) | copy-start | bytes 1769476
  66.7 13.9 %copy-start.5 = (f32[31]{0:T(128)S(1)}, f32[31]{0:T(128)}, u32[]{:S(2)}) copy-start(f32[31]{0:T(128)} %param.19) | copy-start | bytes 376
  67.5 3.7 %collective-permute-start = (f32[15,384]{1,0:T(8,128)S(1)}, f32[15,384]{1,0:T(8,128)S(1)}, u32[]{:S(2)}, u32[]{:S(2)}) collective-permute-start(f32[15,384]{1,0:T(8,128)S(1)} %get-tuple-element.18), channel_id=1, source_target_pairs={{0,8},{8,16},{16,24},{1,9},{9,17},{17,25},{2,10},{10,18},{18,26},{... | collective-permute-start | bytes 69128 | tf_op jit(solution)/shard_map/ppermute | solution.py:25
  69.8 4.6 %collective-permute-start.1 = (f32[15,384]{1,0:T(8,128)S(1)}, f32[15,384]{1,0:T(8,128)S(1)}, u32[]{:S(2)}, u32[]{:S(2)}) collective-permute-start(f32[15,384]{1,0:T(8,128)S(1)} %get-tuple-element.19), channel_id=1, source_target_pairs={{8,0},{16,8},{24,16},{9,1},{17,9},{25,17},{10,2},{18,10},{26,18},{... | collective-permute-start | bytes 69128 | tf_op jit(solution)/shard_map/ppermute | solution.py:26
  74.5 8.1 %collective-permute-start.2 = (f32[414,15]{1,0:T(8,128)S(1)}, f32[414,15]{1,0:T(8,128)S(1)}, u32[]{:S(2)}, u32[]{:S(2)}) collective-permute-start(f32[414,15]{1,0:T(8,128)S(1)} %get-tuple-element.16), channel_id=1, source_target_pairs={{0,1},{1,2},{2,3},{3,4},{4,5},{5,6},{6,7},{8,9},{9,10},{10,11},{11... | collective-permute-start | bytes 74528 | tf_op jit(solution)/shard_map/ppermute | solution.py:25
  78.6 7.2 %collective-permute-start.3 = (f32[414,15]{1,0:T(8,128)S(1)}, f32[414,15]{1,0:T(8,128)S(1)}, u32[]{:S(2)}, u32[]{:S(2)}) collective-permute-start(f32[414,15]{1,0:T(8,128)S(1)} %get-tuple-element.17), channel_id=1, source_target_pairs={{1,0},{2,1},{3,2},{4,3},{5,4},{6,5},{7,6},{9,8},{10,9},{11,10},{12... | collective-permute-start | bytes 74528 | tf_op jit(solution)/shard_map/ppermute | solution.py:26

commit v2 on v1

v2 whole, which is shorter than its diff:
```python
import functools

import jax
import jax.numpy as jnp
from jax import lax
from jax.experimental import pallas as pl
from jax.experimental.pallas import tpu as pltpu
from jax.sharding import PartitionSpec as P

DET_R = 15
PATCH = 384
CAP = 2
LANES = 128
MESH = pl.DeviceIdType.MESH
EXACT = lax.Precision.HIGHEST


def prepare_kernel(kinds, owner, exposure, row_offset, col_offset, weights, coef_table, picks_out, told_out, coef_out):
    count = owner.shape[1]
    entries = weights.shape[1]
    slots = coef_out.shape[0]
    owners = slots // CAP
    at_sub = lax.broadcasted_iota(jnp.int32, (count, count), 0)
    at_lane = lax.broadcasted_iota(jnp.int32, (count, count), 1)

    def column(row):
        spread = jnp.broadcast_to(row, (count, count))
        return jnp.sum(jnp.where(at_sub == at_lane, spread, 0), axis=1, keepdims=True)

    same = jnp.where((column(owner[...]) == owner[...]) & (at_sub < at_lane), 1, 0)
    slot = owner[...] * CAP + jnp.sum(same, axis=0, keepdims=True)
    at_slot = lax.broadcasted_iota(jnp.int32, (count, slots), 1) == column(slot)
    numbers = lax.broadcasted_iota(jnp.int32, (count, slots), 0)
    picks_out[...] = jnp.sum(jnp.where(at_slot, numbers, 0), axis=0, keepdims=True)
    lane = lax.broadcasted_iota(jnp.int32, (owners, LANES), 1)
    told = jnp.zeros((owners, LANES), jnp.int32)
    for j in range(CAP):
        own = lax.broadcasted_iota(jnp.int32, (owners, count), 0) * CAP + j == slot
        values = (jnp.ones_like(slot), exposure[...], row_offset[...], col_offset[...])
        for n, value in enumerate(values):
            found = jnp.sum(jnp.where(own, value, 0), axis=1, keepdims=True)
            told = jnp.where(lane == 4 * j + n, found, told)
    for o in range(owners):
        told_out[o] = told[o : o + 1, :]
    own = lax.broadcasted_iota(jnp.int32, (slots, count), 0) == slot
    index = jnp.sum(jnp.where(own, exposure[...], 0), axis=1, keepdims=True)
    hits = lax.broadcasted_iota(jnp.int32, (slots, entries), 1) == index
    weight = jnp.sum(jnp.where(hits, weights[...], 0.0), axis=1, keepdims=True)
    weight = weight.astype(jnp.bfloat16).astype(jnp.float32)
    width = coef_out.shape[1]
    part = width // (kinds + 1)
    spread = (
        lax.broadcasted_iota(jnp.int32, (kinds, width), 0)
        == lax.broadcasted_iota(jnp.int32, (kinds, width), 1) // part
    ).astype(jnp.float32)
    coefs = lax.dot_general(
        hits.astype(jnp.float32),
        coef_table[...],
        (((1,), (1,)), ((), ())),
        precision=EXACT,
        preferred_element_type=jnp.float32,
    )
    coefs = jnp.dot(coefs, spread, precision=EXACT, preferred_element_type=jnp.float32)
    last = lax.broadcasted_iota(jnp.int32, (slots, width), 1) >= kinds * part
    coef_out[...] = jnp.where(last, weight, coefs)


def build_tables(basis_rows, basis_cols, col_out, row_out):
    kinds, taps = basis_rows.shape
    half = taps // 2
    rows, cols = row_out.shape[0], col_out.shape[0]
    tap = lax.broadcasted_iota(jnp.int32, (taps, LANES), 0)
    lane = lax.broadcasted_iota(jnp.int32, (taps, LANES), 1)

    def spread(value, target):
        hot = jnp.where(lane == (target + LANES) % LANES, 1.0, 0.0).astype(jnp.bfloat16)
        return jnp.dot(value[...], hot, preferred_element_type=jnp.float32)

    col_src = spread(basis_cols, half - tap)
    even = spread(basis_rows, tap - half)
    odd = spread(basis_rows, tap - half + rows)
    near = jnp.abs(
        lax.broadcasted_iota(jnp.int32, (cols, LANES), 1)
        - lax.broadcasted_iota(jnp.int32, (cols, LANES), 0)
    )
    for k in range(kinds):
        source = jnp.broadcast_to(col_src[k : k + 1, :], (cols, LANES))
        rolled = pltpu.roll(source, 0, 1, stride=1, stride_axis=0)
        col_out[:, k * LANES : (k + 1) * LANES] = jnp.where(near <= half, rolled, 0.0).astype(
            jnp.bfloat16
        )
    near = jnp.abs(
        lax.broadcasted_iota(jnp.int32, (rows, LANES), 1) % rows
        - lax.broadcasted_iota(jnp.int32, (rows, LANES), 0)
    )
    for k in range(0, kinds, 2):
        source = even[k : k + 1, :]
        if k + 1 < kinds:
            source = source + odd[k + 1 : k + 2, :]
        rolled = pltpu.roll(
            jnp.broadcast_to(source, (rows, LANES)), 0, 1, stride=1, stride_axis=0
        )
        row_out[:, k * rows : k * rows + LANES] = jnp.where(near <= half, rolled, 0.0)


def route_kernel(
    owners,
    ncol,
    kinds,
    picks,
    blocks,
    coefs,
    info,
    basis_rows,
    basis_cols,
    pixels_out,
    info_out,
    outgoing,
    col_table,
    row_table,
    sems,
):
    me = lax.axis_index("prow") * ncol + lax.axis_index("pcol")
    rows, cols = blocks.shape[1:]
    barrier = pltpu.get_barrier_semaphore()

    def place(device):
        return (device // ncol, device % ncol)

    def greet(i, carry):
        other = lax.rem(me + i, owners)
        pl.semaphore_signal(barrier, inc=1, device_id=place(other), device_id_type=MESH)
        return carry

    lax.fori_loop(1, owners, greet, 0)
    build_tables(basis_rows, basis_cols, col_table, row_table)
    pl.semaphore_wait(barrier, owners - 1)

    def tell(i, carry):
        other = lax.rem(me + i, owners)
        pltpu.make_async_remote_copy(
            src_ref=info.at[other],
            dst_ref=info_out.at[me],
            send_sem=sems.at[0],
            recv_sem=sems.at[1],
            device_id=place(other),
            device_id_type=MESH,
        ).start()
        return carry

    lax.fori_loop(1, owners, tell, 0)
    info_out[me] = info[me]

    group = 4
    step = 4

    def matched_group(first):
        slots_of = [
            lax.rem(first + n, owners) * CAP + j for n in range(group) for j in range(CAP)
        ]
        pixels = jnp.concatenate([blocks[picks[0, s]] for s in slots_of], axis=0)
        coefs_of = [coefs[pl.ds(s, 1), :] for s in slots_of]
        totals = [jnp.zeros((rows, cols), jnp.float32) for _ in slots_of]
        for k in range(0, kinds, step):
            more = min(step, kinds - k)
            section = jnp.dot(
                pixels,
                col_table[:, k * cols : (k + more) * cols],
                preferred_element_type=jnp.float32,
            ).astype(jnp.bfloat16)
            base = row_table[:, k * rows : (k + more) * rows]
            for j in range(len(slots_of)):
                stacked = jnp.concatenate(
                    [
                        section[j * rows : (j + 1) * rows, m * cols : (m + 1) * cols]
                        for m in range(more)
                    ],
                    axis=0,
                )
                coef = coefs_of[j][:, k * rows : (k + more) * rows]
                scaled = (coef * base).astype(jnp.bfloat16)
                totals[j] = totals[j] + jnp.dot(
                    scaled, stacked, preferred_element_type=jnp.float32
                )
        for n in range(group):
            for j in range(CAP):
                s = n * CAP + j
                weight = coefs_of[s][:, kinds * rows : kinds * rows + 1]
                matched = totals[s].astype(jnp.bfloat16).astype(jnp.float32)
                outgoing[lax.rem(first + n, owners), j * rows : (j + 1) * rows, :] = (
                    weight * matched
                ).astype(jnp.bfloat16)

    def send(g, carry):
        matched_group(me + g * group)
        for n in range(group):
            other = lax.rem(me + g * group + n, owners)

            @pl.when(g * group + n > 0)
            def _():
                pltpu.make_async_remote_copy(
                    src_ref=outgoing.at[other],
                    dst_ref=pixels_out.at[me],
                    send_sem=sems.at[2],
                    recv_sem=sems.at[3],
                    device_id=place(other),
                    device_id_type=MESH,
                ).start()

        return carry

    lax.fori_loop(0, owners // group, send, 0)
    pixels_out[me] = outgoing[me]
    others = pl.ds(0, owners - 1)
    for ref, pair in ((info, 0), (outgoing, 2)):
        for which in range(2):
            pltpu.make_async_copy(ref.at[others], ref.at[others], sems.at[pair + which]).wait()


def place_kernel(slots, rows, told, weights, pixels, coadd, total, row_weight, col_cover):
    total[...] = jnp.zeros_like(total)
    cols = pixels.shape[2]
    lane = lax.broadcasted_iota(jnp.int32, (rows, cols), 1)
    span = lax.broadcasted_iota(jnp.int32, (1, PATCH), 1)

    def add(o, carry):
        for j in range(CAP):
            s = o * CAP + j
            live = told[o, 0, 4 * j]
            exposure = told[o, 0, 4 * j + 1]
            row = told[o, 0, 4 * j + 2]
            col = told[o, 0, 4 * j + 3]
            tile = col // cols
            shift = col - tile * cols
            block = pltpu.roll(pixels[s].astype(jnp.float32), shift, 1)
            keep = jnp.where(live > 0, cols, 0)
            here = pl.ds(row, rows)
            left = lane >= shift
            total[tile, here, :] += jnp.where(left & (lane < keep), block, 0.0)
            total[tile + 1, here, :] += jnp.where(left | (lane >= keep), 0.0, block)
            weight = jnp.where(live > 0, weights[exposure], 0.0)
            row_weight[pl.ds(s, 1), :] = jnp.where((span >= row) & (span < row + rows), weight, 0.0)
            col_cover[pl.ds(s, 1), :] = jnp.where((span >= col) & (span < col + cols), 1.0, 0.0)
        return carry

    lax.fori_loop(0, slots // CAP, add, 0)
    depth = lax.dot_general(
        row_weight[...].astype(jnp.bfloat16),
        col_cover[...].astype(jnp.bfloat16),
        (((0,), (0,)), ((), ())),
        preferred_element_type=jnp.float32,
    )
    value = jnp.concatenate([total[t] for t in range(PATCH // cols)], axis=1)
    coadd[...] = value / jnp.maximum(depth, 1.0)


HALO = 16
WIDE = 512


def split_dot(left, right, dims):
    def parts(value):
        high = value.astype(jnp.bfloat16)
        return high, (value - high.astype(jnp.float32)).astype(jnp.bfloat16)

    (a, b), (c, d) = parts(left), parts(right)
    dot = functools.partial(
        lax.dot_general, dimension_numbers=(dims, ((), ())), preferred_element_type=jnp.float32
    )
    return dot(a, c) + (dot(a, d) + dot(b, c))


def detect_kernel(nrow, ncol, coadd, taps, detection, image, halo, sems):
    prow, pcol = lax.axis_index("prow"), lax.axis_index("pcol")
    top, bottom = pl.ds(0, HALO), pl.ds(PATCH - HALO, HALO)
    first, last, whole = pl.ds(0, LANES), pl.ds(PATCH - LANES, LANES), pl.ds(0, PATCH)
    left_tile, right_tile = pl.ds(PATCH, LANES), pl.ds(PATCH + LANES, LANES)
    below = pl.ds(HALO, HALO)
    moves = (
        (0, -1, image.at[below, whole], image.at[pl.ds(PATCH + HALO, HALO), whole]),
        (0, 1, image.at[pl.ds(PATCH, HALO), whole], image.at[top, whole]),
        (1, 0, coadd.at[bottom, whole], halo.at[top, whole]),
        (-1, 0, coadd.at[top, whole], halo.at[below, whole]),
        (1, 1, coadd.at[bottom, last], halo.at[top, left_tile]),
        (1, -1, coadd.at[bottom, first], halo.at[top, right_tile]),
        (-1, 1, coadd.at[top, last], halo.at[below, left_tile]),
        (-1, -1, coadd.at[top, first], halo.at[below, right_tile]),
    )

    def inside(dp, dc):
        row, col = prow + dp, pcol + dc
        return (row >= 0) & (row < nrow) & (col >= 0) & (col < ncol)

    halo[...] = jnp.zeros_like(halo)
    image[0:HALO, :] = jnp.zeros((HALO, WIDE), jnp.float32)
    image[PATCH + HALO :, :] = jnp.zeros((WIDE - PATCH - HALO, WIDE), jnp.float32)
    barrier = pltpu.get_barrier_semaphore()
    count = 0
    for dp, dc, _, _ in moves:
        count = count + jnp.where(inside(dp, dc), 1, 0)

        @pl.when(inside(dp, dc))
        def _():
            pl.semaphore_signal(
                barrier, inc=1, device_id=(prow + dp, pcol + dc), device_id_type=MESH
            )

    image[HALO : HALO + PATCH, 0:PATCH] = coadd[...].T
    pl.semaphore_wait(barrier, count)

    def copy(n):
        dp, dc, source, target = moves[n]
        return pltpu.make_async_remote_copy(
            src_ref=source,
            dst_ref=target,
            send_sem=sems.at[0, n],
            recv_sem=sems.at[1, n],
            device_id=(prow + dp, pcol + dc),
            device_id_type=MESH,
        )

    for n, (dp, dc, _, _) in enumerate(moves):

        @pl.when(inside(dp, dc))
        def _():
            copy(n).start()

    def band(shift):
        source = jnp.broadcast_to(taps[shift : shift + 1, :], (PATCH, WIDE))
        return pltpu.roll(source, 0, 1, stride=1, stride_axis=0)

    across = band(0)
    lane = lax.broadcasted_iota(jnp.int32, (PATCH, LANES), 1)
    edges = jnp.where(
        lane < HALO,
        across[:, 0:LANES],
        jnp.where(lane < 2 * HALO, across[:, PATCH:], 0.0),
    )
    down = jnp.concatenate([band(1)[:, 0:PATCH], edges], axis=1)

    for n, (dp, dc, _, _) in enumerate(moves):

        @pl.when(inside(dp, dc))
        def _():
            copy(n).wait_send()

        @pl.when(inside(-dp, -dc))
        def _():
            copy(n).wait_recv()

    turned = halo[...].T
    image[HALO : HALO + PATCH, PATCH:] = turned[0:PATCH, :]
    image[0:HALO, PATCH:] = turned[PATCH + LANES - HALO : PATCH + LANES, :]
    image[PATCH + HALO : PATCH + 2 * HALO, PATCH:] = turned[PATCH + LANES : PATCH + LANES + HALO, :]
    partial = split_dot(across, image[...], ((1,), (0,)))
    detection[...] = split_dot(down, partial, ((1,), (1,)))


def shards(
    blocks,
    owner,
    row_offset,
    col_offset,
    exposure,
    basis_rows,
    basis_cols,
    coef_table,
    weight_table,
    det_taps,
):
    nrow = lax.axis_size("prow")
    ncol = lax.axis_size("pcol")
    owners = nrow * ncol
    count, rows, cols = blocks.shape
    kinds, taps = basis_rows.shape
    slots = owners * CAP
    vmem = pl.BlockSpec(memory_space=pltpu.VMEM)
    smem = pl.BlockSpec(memory_space=pltpu.SMEM)

    picks, told, coefs = pl.pallas_call(
        functools.partial(prepare_kernel, kinds),
        out_shape=(
            jax.ShapeDtypeStruct((1, slots), jnp.int32),
            jax.ShapeDtypeStruct((owners, 1, LANES), jnp.int32),
            jax.ShapeDtypeStruct((slots, (kinds + 1) * rows), jnp.float32),
        ),
        in_specs=[vmem] * 6,
        out_specs=(vmem,) * 3,
        name="prepare",
    )(
        owner.reshape(1, count),
        exposure[None],
        row_offset[None],
        col_offset[None],
        weight_table[None],
        coef_table.T,
    )

    pixels, heard = pl.pallas_call(
        functools.partial(route_kernel, owners, ncol, kinds),
        out_shape=(
            jax.ShapeDtypeStruct((owners, CAP * rows, cols), jnp.bfloat16),
            jax.ShapeDtypeStruct((owners, 1, LANES), jnp.int32),
        ),
        in_specs=[smem] + [vmem] * 5,
        out_specs=(vmem, vmem),
        scratch_shapes=[
            pltpu.VMEM((owners, CAP * rows, cols), jnp.bfloat16),
            pltpu.VMEM((cols, kinds * cols), jnp.bfloat16),
            pltpu.VMEM((rows, (kinds + kinds % 2) * rows), jnp.float32),
            pltpu.SemaphoreType.DMA((4,)),
        ],
        compiler_params=pltpu.CompilerParams(
            collective_id=0, has_side_effects=True, vmem_limit_bytes=48 * 1024 * 1024
        ),
        name="route",
    )(picks, blocks, coefs, told, basis_rows, basis_cols)

    rounded = weight_table.astype(jnp.bfloat16).astype(jnp.float32)
    coadd = pl.pallas_call(
        functools.partial(place_kernel, slots, rows),
        out_shape=jax.ShapeDtypeStruct((PATCH, PATCH), jnp.float32),
        in_specs=[smem, smem, vmem],
        out_specs=vmem,
        scratch_shapes=[
            pltpu.VMEM((PATCH // cols + 1, PATCH, cols), jnp.float32),
            pltpu.VMEM((slots, PATCH), jnp.float32),
            pltpu.VMEM((slots, PATCH), jnp.float32),
        ],
        compiler_params=pltpu.CompilerParams(vmem_limit_bytes=48 * 1024 * 1024),
        name="place",
    )(heard, rounded, pixels.reshape(slots, rows, cols))

    reach = det_taps.shape[0]
    low = jnp.pad(det_taps, (1, WIDE - reach - 1))
    sources = jnp.stack([low, jnp.roll(low, -HALO)])
    detection = pl.pallas_call(
        functools.partial(detect_kernel, nrow, ncol),
        out_shape=jax.ShapeDtypeStruct((PATCH, PATCH), jnp.float32),
        in_specs=[vmem] * 2,
        out_specs=vmem,
        scratch_shapes=[
            pltpu.VMEM((WIDE, WIDE), jnp.float32),
            pltpu.VMEM((LANES, PATCH + 2 * LANES), jnp.float32),
            pltpu.SemaphoreType.DMA((2, 8)),
        ],
        compiler_params=pltpu.CompilerParams(
            collective_id=1, has_side_effects=True, vmem_limit_bytes=48 * 1024 * 1024
        ),
        name="detect",
    )(coadd, sources)
    return (coadd, detection)


def solution(mesh):
    in_specs = (
        P(("prow", "pcol"), None, None),
        P(("prow", "pcol"), None),
        P(("prow", "pcol")),
        P(("prow", "pcol")),
        P(("prow", "pcol")),
        P(),
        P(),
        P(),
        P(),
        P(),
    )
    out_specs = (P("prow", "pcol"), P("prow", "pcol"))
    return jax.shard_map(shards, mesh=mesh, in_specs=in_specs, out_specs=out_specs, check_vma=False)
```

time: 91.1 us -> 56.5 us (0.62)
  starting transfers between devices: 9.63 us -> 0 us
  other arithmetic: 6.67 us -> 0.09 us
  waiting for transfers between devices: 6.42 us -> 0 us
  matrix products: 4.66 us -> 0 us
  local copies, waits for them, and re-layouts: 11.3 us -> 6.9 us
  Pallas kernels: 51 us -> 48.2 us
    pallas_call x1, Pallas kernels: 41.3 us -> 28.4 us  [shards(): pl.pallas_call(functools.partial(route_kernel, owners, ncol, kinds), out_...]
    pallas_call x1 -> x2, Pallas kernels: 2.94 us -> 14.7 us  [the longest x1 12.3 us: shards(): pl.pallas_call(functools.partial(detect_kernel, nrow, ncol), out_shape=ja...]
    ppermute x4 -> x0, starting transfers between devices: 9.63 us -> none  [the longest x2 6.42 us: padded_2(): before = lax.ppermute(last, axis, up)]
    ppermute x4 -> x0, waiting for transfers between devices: 6.42 us -> none  [the longest x2 6.42 us: padded_2(): after = lax.ppermute(leading, axis, down)]
    dot_general x2 -> x0, matrix products: 4.66 us -> none  [the longest x1 2.35 us: detect(): return jnp.dot(across, band.T, precision=EXACT)]
    slice x8 -> x2, local copies, waits for them, and re-layouts: 2.86 us -> 0.15 us  [shards(): sources = jnp.stack([low, jnp.roll(low, -HALO)])]
    unnamed x13 -> x19, local copies, waits for them, and re-layouts: 4.43 us -> 6.68 us
    concatenate x3 -> x1, other arithmetic: 2.1 us -> 0.08 us  [shards(): sources = jnp.stack([low, jnp.roll(low, -HALO)])]
  transfers between devices with their start and end apart: 4 -> 0, of which waited for: 2 -> 0; matrix products, arithmetic and copies ran while one was open for 2% -> 0% of each run, Pallas kernels for 0% -> 0%
where the time goes in v2:
time: 56.5 us; the launch traced here: 55.9 us
  Pallas kernels  48.2 us (85%)
  local copies, waits for them, and re-layouts  6.9 us (12%)
  between operations  0.68 us (1%)
    pallas_call x1, Pallas kernels, shards(): pl.pallas_call(functools.partial(route_kernel, owners, ncol, kinds), out_...  28.4 us
    pallas_call x1, Pallas kernels, shards(): pl.pallas_call(functools.partial(detect_kernel, nrow, ncol), out_shape=ja...  12.3 us
    unnamed x19, local copies, waits for them, and re-layouts  6.68 us
    pallas_call x1, Pallas kernels, shards(): pl.pallas_call(functools.partial(place_kernel, slots, rows), out_shape=ja...  5.04 us
    pallas_call x1, Pallas kernels, shards(): pl.pallas_call(functools.partial(prepare_kernel, kinds), out_shape=(jax.S...  2.45 us

profile of v2, /device:TPU:1, one launch (start us, length us, event | category | flops | bytes accessed | tf_op | source)
XLA Modules:
  0.0 55.9 jit_solution(16320701000764188065)
XLA Ops:
  0.6 0.0 copy-start.8
  0.6 0.6 %copy-done.8 = f32[31]{0:T(128)S(1)} copy-done((f32[31]{0:T(128)S(1)}, f32[31]{0:T(128)}, u32[]{:S(2)}) %copy-start.8) | copy-done | bytes 148
  1.3 0.0 copy-start.7
  1.3 0.1 pad_slice_fusion
  1.4 0.6 %copy-done.7 = f32[256]{0:T(256)S(1)} copy-done((f32[256]{0:T(256)S(1)}, f32[256]{0:T(256)}, u32[]{:S(2)}) %copy-start.7) | copy-done | bytes 1048
  2.0 0.1 pad_slice_fusion.1
  2.0 0.1 pad_maximum_fusion.1
  2.1 0.1 pad.4
  2.2 0.0 copy-start.4
  2.2 0.0 copy-start.5
  2.2 2.4 %prepare.1 = (s32[1,64]{1,0:T(1,128)}, s32[32,1,128]{2,1,0:T(1,128)}, f32[64,1408]{1,0:T(8,128)}) custom-call(s32[1,64]{1,0:T(1,128)} %bitcast.14, s32[1,64]{1,0:T(1,128)} %bitcast.15, s32[1,64]{1,0:T(1,128)} %bitcast.16, s32[1,64]{1,0:T(1,128)} %bitcast.17, f32[1,256]{1,0:T(1,128)} %bitcast.13, f32[21,256]{1,0:T(8,128)} %bitcast.10), custom_call_target="tpu_custom_call" | custom-call | tf_op jit(solution)/shard_map/prepare/pallas_call | solution.py:380
  4.7 0.0 copy-start.6
  4.7 0.0 copy-done.4
  4.7 0.0 copy-done.5
  4.7 0.6 %copy-done.6 = s32[1,64]{1,0:T(1,128)S(1)} copy-done((s32[1,64]{1,0:T(1,128)S(1)}, s32[1,64]{1,0:T(1,128)}, u32[]{:S(2)}) %copy-start.6) | copy-done | bytes 280
  5.3 0.0 copy-start.1
  5.3 1.2 %copy-done.1 = bf16[64,64,128]{2,1,0:T(8,128)(2,1)S(1)} copy-done((bf16[64,64,128]{2,1,0:T(8,128)(2,1)S(1)}, bf16[64,64,128]{2,1,0:T(8,128)(2,1)}, u32[]{:S(2)}) %copy-start.1) | copy-done | bytes 1048600
  6.5 0.0 copy-start.2
  6.5 1.0 %copy-done.2 = f32[64,1408]{1,0:T(8,128)S(1)} copy-done((f32[64,1408]{1,0:T(8,128)S(1)}, f32[64,1408]{1,0:T(8,128)}, u32[]{:S(2)}) %copy-start.2) | copy-done | bytes 360472
  7.5 0.0 copy-start.3
  7.5 0.7 %copy-done.3 = s32[32,1,128]{2,1,0:T(1,128)S(1)} copy-done((s32[32,1,128]{2,1,0:T(1,128)S(1)}, s32[32,1,128]{2,1,0:T(1,128)}, u32[]{:S(2)}) %copy-start.3) | copy-done | bytes 16408
  8.2 28.4 %route.1 = (bf16[32,128,128]{2,1,0:T(8,128)(2,1)S(1)}, s32[32,1,128]{2,1,0:T(1,128)S(1)}) custom-call(s32[1,64]{1,0:T(1,128)S(1)} %copy-done.6, bf16[64,64,128]{2,1,0:T(8,128)(2,1)S(1)} %copy-done.1, f32[64,1408]{1,0:T(8,128)S(1)} %copy-done.2, s32[32,1,128]{2,1,0:T(1,128)S(1)} %copy-done.3, bf16[21,31]{1,0:T(8,128)(2,1)S(1)} %copy-done.4, ...), custom_call_target="tpu_custom_call" | custom-call | tf_op jit(solution)/shard_map/route/pallas_call | solution.py:399
  36.7 5.0 %place.1.coadd = f32[384,384]{1,0:T(8,128)} custom-call(s32[32,1,128]{2,1,0:T(1,128)S(1)} %get-tuple-element.10.told, f32[256]{0:T(256)S(1)} %convert_convert_fusion.weights, bf16[64,64,128]{2,1,0:T(8,128)(2,1)S(1)} %bitcast.9), custom_call_target="tpu_custom_call" | custom-call | tf_op jit(solution)/shard_map/place/pallas_call | solution.py:420
  41.7 0.0 copy-start
  41.7 1.1 %copy-done = f32[384,384]{1,0:T(8,128)S(1)} copy-done((f32[384,384]{1,0:T(8,128)S(1)}, f32[384,384]{1,0:T(8,128)}, u32[]{:S(2)}) %copy-start) | copy-done | bytes 589848
  42.8 12.3 %detect.1 = f32[384,384]{1,0:T(8,128)S(1)} custom-call(f32[384,384]{1,0:T(8,128)S(1)} %copy-done, f32[2,512]{1,0:T(2,128)S(1)} %pad_maximum_fusion.taps), custom_call_target="tpu_custom_call" | custom-call | tf_op jit(solution)/shard_map/detect/pallas_call | solution.py:437
  55.1 0.8 %copy.13 = f32[384,384]{1,0:T(8,128)} copy(f32[384,384]{1,0:T(8,128)S(1)} %detect.1) | data formatting | bytes 1179648
  (2 shorter events, 0.0 us)
Async XLA Ops:
  0.6 0.7 %copy-start.8 = (f32[31]{0:T(128)S(1)}, f32[31]{0:T(128)}, u32[]{:S(2)}) copy-start(f32[31]{0:T(128)} %param.19) | copy-start | bytes 376
  1.3 0.7 %copy-start.7 = (f32[256]{0:T(256)S(1)}, f32[256]{0:T(256)}, u32[]{:S(2)}) copy-start(f32[256]{0:T(256)} %param.18) | copy-start | bytes 3076
  2.2 2.5 %copy-start.4 = (bf16[21,31]{1,0:T(8,128)(2,1)S(1)}, bf16[21,31]{1,0:T(8,128)(2,1)}, u32[]{:S(2)}) copy-start(bf16[21,31]{1,0:T(8,128)(2,1)} %basis_rows.1) | copy-start | bytes 3910
  2.2 2.5 %copy-start.5 = (bf16[21,31]{1,0:T(8,128)(2,1)S(1)}, bf16[21,31]{1,0:T(8,128)(2,1)}, u32[]{:S(2)}) copy-start(bf16[21,31]{1,0:T(8,128)(2,1)} %basis_cols.1) | copy-start | bytes 3910
  4.7 0.6 %copy-start.6 = (s32[1,64]{1,0:T(1,128)S(1)}, s32[1,64]{1,0:T(1,128)}, u32[]{:S(2)}) copy-start(s32[1,64]{1,0:T(1,128)} %get-tuple-element.7.picks) | copy-start | bytes 772
  5.3 1.2 %copy-start.1 = (bf16[64,64,128]{2,1,0:T(8,128)(2,1)S(1)}, bf16[64,64,128]{2,1,0:T(8,128)(2,1)}, u32[]{:S(2)}) copy-start(bf16[64,64,128]{2,1,0:T(8,128)(2,1)} %blocks.1) | copy-start | bytes 3145732
  6.5 1.0 %copy-start.2 = (f32[64,1408]{1,0:T(8,128)S(1)}, f32[64,1408]{1,0:T(8,128)}, u32[]{:S(2)}) copy-start(f32[64,1408]{1,0:T(8,128)} %get-tuple-element.8.coefs) | copy-start | bytes 1081348
  7.5 0.7 %copy-start.3 = (s32[32,1,128]{2,1,0:T(1,128)S(1)}, s32[32,1,128]{2,1,0:T(1,128)}, u32[]{:S(2)}) copy-start(s32[32,1,128]{2,1,0:T(1,128)} %get-tuple-element.9.info) | copy-start | bytes 49156
  41.7 1.1 %copy-start = (f32[384,384]{1,0:T(8,128)S(1)}, f32[384,384]{1,0:T(8,128)}, u32[]{:S(2)}) copy-start(f32[384,384]{1,0:T(8,128)} %place.1.coadd) | copy-start | bytes 1769476

commit v3 on v2

v3 whole, which is shorter than its diff:
```python
import functools

import jax
import jax.numpy as jnp
from jax import lax
from jax.experimental import pallas as pl
from jax.experimental.pallas import tpu as pltpu
from jax.sharding import PartitionSpec as P

DET_R = 15
PATCH = 384
CAP = 2
LANES = 128
MESH = pl.DeviceIdType.MESH
EXACT = lax.Precision.HIGHEST


HALO = 16
WIDE = 512


def split_dot(left, right, dims):
    def parts(value):
        high = value.astype(jnp.bfloat16)
        return high, (value - high.astype(jnp.float32)).astype(jnp.bfloat16)

    (a, b), (c, d) = parts(left), parts(right)
    dot = functools.partial(
        lax.dot_general, dimension_numbers=(dims, ((), ())), preferred_element_type=jnp.float32
    )
    return dot(a, c) + (dot(a, d) + dot(b, c))


def prepare(kinds, owner, exposure, row_offset, col_offset, weights, coef_table, picks_out, told_out, coef_out):
    count = owner.shape[1]
    entries = weights.shape[1]
    slots = coef_out.shape[0]
    owners = slots // CAP
    at_sub = lax.broadcasted_iota(jnp.int32, (count, count), 0)
    at_lane = lax.broadcasted_iota(jnp.int32, (count, count), 1)

    def column(row):
        spread = jnp.broadcast_to(row, (count, count))
        return jnp.sum(jnp.where(at_sub == at_lane, spread, 0), axis=1, keepdims=True)

    same = jnp.where((column(owner[...]) == owner[...]) & (at_sub < at_lane), 1, 0)
    slot = owner[...] * CAP + jnp.sum(same, axis=0, keepdims=True)
    at_slot = lax.broadcasted_iota(jnp.int32, (count, slots), 1) == column(slot)
    numbers = lax.broadcasted_iota(jnp.int32, (count, slots), 0)
    picks_out[...] = jnp.sum(jnp.where(at_slot, numbers, 0), axis=0, keepdims=True)
    lane = lax.broadcasted_iota(jnp.int32, (owners, LANES), 1)
    told = jnp.zeros((owners, LANES), jnp.int32)
    for j in range(CAP):
        own = lax.broadcasted_iota(jnp.int32, (owners, count), 0) * CAP + j == slot
        values = (jnp.ones_like(slot), exposure[...], row_offset[...], col_offset[...])
        for n, value in enumerate(values):
            found = jnp.sum(jnp.where(own, value, 0), axis=1, keepdims=True)
            told = jnp.where(lane == 4 * j + n, found, told)
    for o in range(owners):
        told_out[o] = told[o : o + 1, :]
    own = lax.broadcasted_iota(jnp.int32, (slots, count), 0) == slot
    index = jnp.sum(jnp.where(own, exposure[...], 0), axis=1, keepdims=True)
    hits = lax.broadcasted_iota(jnp.int32, (slots, entries), 1) == index
    weight = jnp.sum(jnp.where(hits, weights[...], 0.0), axis=1, keepdims=True)
    weight = weight.astype(jnp.bfloat16).astype(jnp.float32)
    width = coef_out.shape[1]
    part = width // (kinds + 1)
    spread = (
        lax.broadcasted_iota(jnp.int32, (kinds, width), 0)
        == lax.broadcasted_iota(jnp.int32, (kinds, width), 1) // part
    ).astype(jnp.float32)
    coefs = lax.dot_general(
        hits.astype(jnp.float32),
        coef_table[...],
        (((1,), (1,)), ((), ())),
        precision=EXACT,
        preferred_element_type=jnp.float32,
    )
    coefs = jnp.dot(coefs, spread, precision=EXACT, preferred_element_type=jnp.float32)
    last = lax.broadcasted_iota(jnp.int32, (slots, width), 1) >= kinds * part
    coef_out[...] = jnp.where(last, weight, coefs)


def build_tables(basis_rows, basis_cols, col_out, row_out):
    kinds, taps = basis_rows.shape
    half = taps // 2
    rows, cols = row_out.shape[0], col_out.shape[0]
    tap = lax.broadcasted_iota(jnp.int32, (taps, LANES), 0)
    lane = lax.broadcasted_iota(jnp.int32, (taps, LANES), 1)

    def spread(value, target):
        hot = jnp.where(lane == (target + LANES) % LANES, 1.0, 0.0).astype(jnp.bfloat16)
        return jnp.dot(value[...], hot, preferred_element_type=jnp.float32)

    col_src = spread(basis_cols, half - tap)
    even = spread(basis_rows, tap - half)
    odd = spread(basis_rows, tap - half + rows)
    near = jnp.abs(
        lax.broadcasted_iota(jnp.int32, (cols, LANES), 1)
        - lax.broadcasted_iota(jnp.int32, (cols, LANES), 0)
    )
    for k in range(kinds):
        source = jnp.broadcast_to(col_src[k : k + 1, :], (cols, LANES))
        rolled = pltpu.roll(source, 0, 1, stride=1, stride_axis=0)
        col_out[:, k * LANES : (k + 1) * LANES] = jnp.where(near <= half, rolled, 0.0).astype(
            jnp.bfloat16
        )
    near = jnp.abs(
        lax.broadcasted_iota(jnp.int32, (rows, LANES), 1) % rows
        - lax.broadcasted_iota(jnp.int32, (rows, LANES), 0)
    )
    for k in range(0, kinds, 2):
        source = even[k : k + 1, :]
        if k + 1 < kinds:
            source = source + odd[k + 1 : k + 2, :]
        rolled = pltpu.roll(
            jnp.broadcast_to(source, (rows, LANES)), 0, 1, stride=1, stride_axis=0
        )
        row_out[:, k * rows : k * rows + LANES] = jnp.where(near <= half, rolled, 0.0)


def whole_kernel(
    nrow,
    ncol,
    owner,
    exposure,
    row_offset,
    col_offset,
    weights,
    coef_table,
    basis_rows,
    basis_cols,
    taps,
    source_blocks,
    coadd,
    detection,
    blocks,
    pick_row,
    picks,
    info,
    coefs,
    col_table,
    row_table,
    outgoing,
    arrived,
    heard,
    total,
    image,
    halo,
    sems,
    data_sems,
    halo_sems,
):
    owners = nrow * ncol
    prow, pcol = lax.axis_index("prow"), lax.axis_index("pcol")
    me = prow * ncol + pcol
    rows, cols = blocks.shape[1:]
    kinds = basis_rows.shape[0]
    span = nrow // 2 if nrow % 2 == 0 else nrow

    def turn(i):
        step, col = i // ncol, (pcol + 1 + i) % ncol
        side = (prow // span + 1 + step // span) % (nrow // span)
        return (side * span + (prow + 1 + step) % span) * ncol + col

    def source(i):
        step, col = i // ncol, (pcol + 2 * ncol - 1 - i % ncol) % ncol
        side = (prow // span + 1 + step // span) % (nrow // span)
        return (side * span + (prow + 2 * span - 1 - step % span) % span) * ncol + col

    def place(device):
        return (device // ncol, device % ncol)

    load = pltpu.make_async_copy(source_blocks, blocks, sems.at[3])
    load.start()
    halo[...] = jnp.zeros_like(halo)
    image[0:HALO, :] = jnp.zeros((HALO, WIDE), jnp.float32)
    image[PATCH + HALO :, :] = jnp.zeros((WIDE - PATCH - HALO, WIDE), jnp.float32)
    barrier = pltpu.get_barrier_semaphore()

    def greet(i, carry):
        other = lax.rem(me + i, owners)
        pl.semaphore_signal(barrier, inc=1, device_id=place(other), device_id_type=MESH)
        return carry

    lax.fori_loop(1, owners, greet, 0)
    prepare(
        kinds, owner, exposure, row_offset, col_offset, weights, coef_table, pick_row, info, coefs
    )
    lift = pltpu.make_async_copy(pick_row, picks, sems.at[2])
    lift.start()
    build_tables(basis_rows, basis_cols, col_table, row_table)
    total[...] = jnp.zeros_like(total)
    lift.wait()
    load.wait()
    pl.semaphore_wait(barrier, owners - 1)

    def tell(i, carry):
        other = lax.rem(me + i, owners)
        pltpu.make_async_remote_copy(
            src_ref=info.at[other],
            dst_ref=heard.at[me],
            send_sem=sems.at[0],
            recv_sem=sems.at[1],
            device_id=place(other),
            device_id_type=MESH,
        ).start()
        return carry

    lax.fori_loop(1, owners, tell, 0)
    heard[me] = info[me]

    group = 2
    step = 4

    def matched_group(first):
        slots_of = [
            turn(first + n) * CAP + j for n in range(group) for j in range(CAP)
        ]
        pixels = jnp.concatenate([blocks[picks[0, s]] for s in slots_of], axis=0)
        coefs_of = [coefs[pl.ds(s, 1), :] for s in slots_of]
        totals = [jnp.zeros((rows, cols), jnp.float32) for _ in slots_of]
        for k in range(0, kinds, step):
            more = min(step, kinds - k)
            section = jnp.dot(
                pixels,
                col_table[:, k * cols : (k + more) * cols],
                preferred_element_type=jnp.float32,
            ).astype(jnp.bfloat16)
            base = row_table[:, k * rows : (k + more) * rows]
            for j in range(len(slots_of)):
                stacked = jnp.concatenate(
                    [
                        section[j * rows : (j + 1) * rows, m * cols : (m + 1) * cols]
                        for m in range(more)
                    ],
                    axis=0,
                )
                coef = coefs_of[j][:, k * rows : (k + more) * rows]
                scaled = (coef * base).astype(jnp.bfloat16)
                totals[j] = totals[j] + jnp.dot(
                    scaled, stacked, preferred_element_type=jnp.float32
                )
        for n in range(group):
            for j in range(CAP):
                s = n * CAP + j
                weight = coefs_of[s][:, kinds * rows : kinds * rows + 1]
                matched = totals[s].astype(jnp.bfloat16).astype(jnp.float32)
                outgoing[turn(first + n), j * rows : (j + 1) * rows, :] = (
                    weight * matched
                ).astype(jnp.bfloat16)

    def data_copy(other, origin):
        return pltpu.make_async_remote_copy(
            src_ref=outgoing.at[other],
            dst_ref=arrived.at[origin],
            send_sem=data_sems.at[0, other],
            recv_sem=data_sems.at[1, origin],
            device_id=place(other),
            device_id_type=MESH,
        )

    def send(g, carry):
        matched_group(g * group)
        for n in range(group):
            other = turn(g * group + n)

            @pl.when(g * group + n < owners - 1)
            def _():
                data_copy(other, me).start()

        return carry

    lax.fori_loop(0, owners // group, send, 0)
    arrived[me] = outgoing[me]
    others = pl.ds(0, owners - 1)
    for which in range(2):
        pltpu.make_async_copy(info.at[others], info.at[others], sems.at[which]).wait()

    wide = lax.broadcasted_iota(jnp.int32, (owners, PATCH), 1)
    entries = weights.shape[1]
    letters = jnp.concatenate([heard[o] for o in range(owners)], axis=0)
    depth = jnp.zeros((PATCH, PATCH), jnp.float32)
    for j in range(CAP):
        live, entry, top, left = (letters[:, 4 * j + n : 4 * j + n + 1] for n in range(4))
        hits = lax.broadcasted_iota(jnp.int32, (owners, entries), 1) == entry
        weight = jnp.sum(jnp.where(hits, weights[...], 0.0), axis=1, keepdims=True)
        weight = jnp.where(live > 0, weight, 0.0)
        row_weight = jnp.where((wide >= top) & (wide < top + rows), weight, 0.0)
        col_cover = jnp.where((wide >= left) & (wide < left + cols), 1.0, 0.0)
        depth = depth + lax.dot_general(
            row_weight.astype(jnp.bfloat16),
            col_cover.astype(jnp.bfloat16),
            (((0,), (0,)), ((), ())),
            preferred_element_type=jnp.float32,
        )
    coadd[...] = jnp.maximum(depth, 1.0)

    offset = lax.broadcasted_iota(jnp.int32, (cols, PATCH), 1) - lax.broadcasted_iota(
        jnp.int32, (cols, PATCH), 0
    )
    many = group * CAP
    down = lax.broadcasted_iota(jnp.int32, (PATCH, many * rows), 0)
    lane = lax.broadcasted_iota(jnp.int32, (1, many * rows), 1)

    def gather(g, carry):
        target = lane % rows
        shifted = []
        for n in range(group):
            origin = source(g * group + n)

            @pl.when(g * group + n < owners - 1)
            def _():
                data_copy(origin, origin).wait_recv()

            letter = heard[origin]
            for j in range(CAP):
                live, _, top, left = (letter[:, 4 * j + n : 4 * j + n + 1] for n in range(4))
                hot = jnp.where((offset == left) & (live > 0), 1.0, 0.0).astype(jnp.bfloat16)
                block = arrived[origin, j * rows : (j + 1) * rows, :]
                shifted.append(
                    jnp.dot(block, hot, preferred_element_type=jnp.float32).astype(jnp.bfloat16)
                )
                target = target + jnp.where(lane // rows == n * CAP + j, top, 0)
        hot = jnp.where(down == target, 1.0, 0.0).astype(jnp.bfloat16)
        total[...] += jnp.dot(
            hot, jnp.concatenate(shifted, axis=0), preferred_element_type=jnp.float32
        )
        return carry

    lax.fori_loop(0, owners // group, gather, 0)
    coadd[...] = total[...] / coadd[...]

    first_rows, last_rows = pl.ds(0, HALO), pl.ds(PATCH - HALO, HALO)
    first, last, whole = pl.ds(0, LANES), pl.ds(PATCH - LANES, LANES), pl.ds(0, PATCH)
    left_tile, right_tile = pl.ds(PATCH, LANES), pl.ds(PATCH + LANES, LANES)
    below = pl.ds(HALO, HALO)
    moves = (
        (1, 0, coadd.at[last_rows, whole], halo.at[first_rows, whole]),
        (-1, 0, coadd.at[first_rows, whole], halo.at[below, whole]),
        (1, 1, coadd.at[last_rows, last], halo.at[first_rows, left_tile]),
        (1, -1, coadd.at[last_rows, first], halo.at[first_rows, right_tile]),
        (-1, 1, coadd.at[first_rows, last], halo.at[below, left_tile]),
        (-1, -1, coadd.at[first_rows, first], halo.at[below, right_tile]),
        (0, -1, image.at[below, whole], image.at[pl.ds(PATCH + HALO, HALO), whole]),
        (0, 1, image.at[pl.ds(PATCH, HALO), whole], image.at[first_rows, whole]),
    )

    def inside(dp, dc):
        row, col = prow + dp, pcol + dc
        return (row >= 0) & (row < nrow) & (col >= 0) & (col < ncol)

    def halo_copy(n):
        dp, dc, origin, target = moves[n]
        return pltpu.make_async_remote_copy(
            src_ref=origin,
            dst_ref=target,
            send_sem=halo_sems.at[0, n],
            recv_sem=halo_sems.at[1, n],
            device_id=(prow + dp, pcol + dc),
            device_id_type=MESH,
        )

    for n, (dp, dc, _, _) in enumerate(moves):
        if dp == 0 and dc < 0:
            image[HALO : HALO + PATCH, 0:PATCH] = coadd[...].T

        @pl.when(inside(dp, dc))
        def _():
            halo_copy(n).start()

    def sent(i, carry):
        other = turn(i)
        data_copy(other, other).wait_send()
        return carry

    lax.fori_loop(0, owners - 1, sent, 0)

    def band(shift):
        origin = jnp.broadcast_to(taps[shift : shift + 1, :], (PATCH, WIDE))
        return pltpu.roll(origin, 0, 1, stride=1, stride_axis=0)

    across = band(0)
    lane = lax.broadcasted_iota(jnp.int32, (PATCH, LANES), 1)
    edges = jnp.where(
        lane < HALO,
        across[:, 0:LANES],
        jnp.where(lane < 2 * HALO, across[:, PATCH:], 0.0),
    )
    along = jnp.concatenate([band(1)[:, 0:PATCH], edges], axis=1)

    for n, (dp, dc, _, _) in enumerate(moves):

        @pl.when(inside(dp, dc))
        def _():
            halo_copy(n).wait_send()

        @pl.when(inside(-dp, -dc))
        def _():
            halo_copy(n).wait_recv()

    turned = halo[...].T
    image[HALO : HALO + PATCH, PATCH:] = turned[0:PATCH, :]
    image[0:HALO, PATCH:] = turned[PATCH + LANES - HALO : PATCH + LANES, :]
    image[PATCH + HALO : PATCH + 2 * HALO, PATCH:] = turned[PATCH + LANES : PATCH + LANES + HALO, :]
    partial = split_dot(across, image[...], ((1,), (0,)))
    detection[...] = split_dot(along, partial, ((1,), (1,)))


def shards(
    blocks,
    owner,
    row_offset,
    col_offset,
    exposure,
    basis_rows,
    basis_cols,
    coef_table,
    weight_table,
    det_taps,
):
    nrow = lax.axis_size("prow")
    ncol = lax.axis_size("pcol")
    owners = nrow * ncol
    count, rows, cols = blocks.shape
    kinds, taps = basis_rows.shape
    slots = owners * CAP
    vmem = pl.BlockSpec(memory_space=pltpu.VMEM)

    reach = det_taps.shape[0]
    low = jnp.pad(det_taps, (1, WIDE - reach - 1))
    bands = jnp.stack([low, jnp.roll(low, -HALO)])
    tract = jax.ShapeDtypeStruct((PATCH, PATCH), jnp.float32)
    even = kinds + kinds % 2
    return pl.pallas_call(
        functools.partial(whole_kernel, nrow, ncol),
        out_shape=(tract, tract),
        in_specs=[vmem] * 9 + [pl.BlockSpec(memory_space=pl.ANY)],
        out_specs=(vmem, vmem),
        scratch_shapes=[
            pltpu.VMEM((count, rows, cols), jnp.bfloat16),
            pltpu.VMEM((1, slots), jnp.int32),
            pltpu.SMEM((1, slots), jnp.int32),
            pltpu.VMEM((owners, 1, LANES), jnp.int32),
            pltpu.VMEM((slots, (kinds + 1) * rows), jnp.float32),
            pltpu.VMEM((cols, kinds * cols), jnp.bfloat16),
            pltpu.VMEM((rows, even * rows), jnp.float32),
            pltpu.VMEM((owners, CAP * rows, cols), jnp.bfloat16),
            pltpu.VMEM((owners, CAP * rows, cols), jnp.bfloat16),
            pltpu.VMEM((owners, 1, LANES), jnp.int32),
            pltpu.VMEM((PATCH, PATCH), jnp.float32),
            pltpu.VMEM((WIDE, WIDE), jnp.float32),
            pltpu.VMEM((LANES, PATCH + 2 * LANES), jnp.float32),
            pltpu.SemaphoreType.DMA((4,)),
            pltpu.SemaphoreType.DMA((2, owners)),
            pltpu.SemaphoreType.DMA((2, 8)),
        ],
        compiler_params=pltpu.CompilerParams(
            collective_id=0, has_side_effects=True, vmem_limit_bytes=56 * 1024 * 1024
        ),
        name="whole",
    )(
        owner.reshape(1, count),
        exposure[None],
        row_offset[None],
        col_offset[None],
        weight_table[None],
        coef_table.T,
        basis_rows,
        basis_cols,
        bands,
        blocks,
    )


def solution(mesh):
    in_specs = (
        P(("prow", "pcol"), None, None),
        P(("prow", "pcol"), None),
        P(("prow", "pcol")),
        P(("prow", "pcol")),
        P(("prow", "pcol")),
        P(),
        P(),
        P(),
        P(),
        P(),
    )
    out_specs = (P("prow", "pcol"), P("prow", "pcol"))
    return jax.shard_map(shards, mesh=mesh, in_specs=in_specs, out_specs=out_specs, check_vma=False)
```

time: 56.5 us -> 51 us (0.903)
  local copies, waits for them, and re-layouts: 6.9 us -> 3.67 us
  Pallas kernels: 48.2 us -> 45.8 us
  other arithmetic: 0.09 us -> 0.68 us
    unnamed x19 -> x6, local copies, waits for them, and re-layouts: 6.68 us -> 3.45 us
    pallas_call x4 -> x1, Pallas kernels: 48.2 us -> 45.8 us  [shards(): pl.pallas_call(functools.partial(whole_kernel, nrow, ncol), out_shape=(tr...]
    another operation x1, other arithmetic: 0.01 us -> 0.6 us  [shards(): bands = jnp.stack([low, jnp.roll(low, -HALO)])]
where the time goes in v3:
time: 51 us; the launch traced here: 50.8 us
  Pallas kernels  45.8 us (90%)
  local copies, waits for them, and re-layouts  3.67 us (7%)
  other arithmetic  0.68 us (1%)
  between operations  0.66 us (1%)
    pallas_call x1, Pallas kernels, shards(): pl.pallas_call(functools.partial(whole_kernel, nrow, ncol), out_shape=(tr...  45.8 us
    unnamed x6, local copies, waits for them, and re-layouts  3.45 us

profile of v3, /device:TPU:1, one launch (start us, length us, event | category | flops | bytes accessed | tf_op | source)
XLA Modules:
  0.0 50.8 jit_solution(7453611273743702618)
XLA Ops:
  0.6 0.0 copy-start.1
  0.6 0.6 %copy-done.1 = f32[31]{0:T(128)S(1)} copy-done((f32[31]{0:T(128)S(1)}, f32[31]{0:T(128)}, u32[]{:S(2)}) %copy-start.1) | copy-done | bytes 148
  1.3 0.1 pad_slice_fusion
  1.4 0.1 pad_slice_fusion.1
  1.4 0.1 pad_maximum_fusion.1
  1.5 0.1 pad.4
  1.6 0.6 %pad_maximum_fusion.taps = f32[2,512]{1,0:T(2,128)} fusion(f32[1,512]{1,0:T(1,128)S(1)} %bitcast.9, f32[1,512]{1,0:T(1,128)S(1)} %bitcast.10), kind=kLoop, calls=%fused_computation | loop fusion | flops 1024 | bytes 8192 | tf_op jit(solution)/shard_map/stack | solution.py:432
  2.2 45.8 %whole.1 = (f32[384,384]{1,0:T(8,128)}, f32[384,384]{1,0:T(8,128)}) custom-call(s32[1,64]{1,0:T(1,128)} %bitcast.12, s32[1,64]{1,0:T(1,128)} %bitcast.13, s32[1,64]{1,0:T(1,128)} %bitcast.14, s32[1,64]{1,0:T(1,128)} %bitcast.15, f32[1,256]{1,0:T(1,128)} %bitcast.11, f32[21,256]{1,0:T(8,128)} %bitcast.8, bf16[21,31]{1,0:T(8,128)(2,1)} %basis_rows.1, ...), custom_call_target="tpu_custom_call" | custom-call | tf_op jit(solution)/shard_map/whole/pallas_call | solution.py:435
  48.0 0.0 copy-start
  48.0 2.0 %copy.14 = f32[384,384]{1,0:T(8,128)} copy(f32[384,384]{1,0:T(8,128)} %get-tuple-element.4) | data formatting | bytes 1179648
  50.0 0.0 copy-done
  50.0 0.8 %copy.15 = f32[384,384]{1,0:T(8,128)} copy(f32[384,384]{1,0:T(8,128)S(1)} %copy-done) | data formatting | bytes 1179648
Async XLA Ops:
  0.6 0.7 %copy-start.1 = (f32[31]{0:T(128)S(1)}, f32[31]{0:T(128)}, u32[]{:S(2)}) copy-start(f32[31]{0:T(128)} %param.19) | copy-start | bytes 376
  48.0 2.0 %copy-start = (f32[384,384]{1,0:T(8,128)S(1)}, f32[384,384]{1,0:T(8,128)}, u32[]{:S(2)}) copy-start(f32[384,384]{1,0:T(8,128)} %get-tuple-element.5) | copy-start | bytes 1769476

commit v4 on v3

--- a/solution.py
+++ b/solution.py
@@ -210,12 +210,12 @@
     lax.fori_loop(1, owners, tell, 0)
     heard[me] = info[me]
 
-    group = 2
+    mgroup = 2
     step = 4
 
     def matched_group(first):
         slots_of = [
-            turn(first + n) * CAP + j for n in range(group) for j in range(CAP)
+            turn(first + n) * CAP + j for n in range(mgroup) for j in range(CAP)
         ]
         pixels = jnp.concatenate([blocks[picks[0, s]] for s in slots_of], axis=0)
         coefs_of = [coefs[pl.ds(s, 1), :] for s in slots_of]
@@ -241,7 +241,7 @@
                 totals[j] = totals[j] + jnp.dot(
                     scaled, stacked, preferred_element_type=jnp.float32
                 )
-        for n in range(group):
+        for n in range(mgroup):
             for j in range(CAP):
                 s = n * CAP + j
                 weight = coefs_of[s][:, kinds * rows : kinds * rows + 1]
@@ -261,17 +261,17 @@
         )
 
     def send(g, carry):
-        matched_group(g * group)
-        for n in range(group):
-            other = turn(g * group + n)
-
-            @pl.when(g * group + n < owners - 1)
+        matched_group(g * mgroup)
+        for n in range(mgroup):
+            other = turn(g * mgroup + n)
+
+            @pl.when(g * mgroup + n < owners - 1)
             def _():
                 data_copy(other, me).start()
 
         return carry
 
-    lax.fori_loop(0, owners // group, send, 0)
+    lax.fori_loop(0, owners // mgroup, send, 0)
     arrived[me] = outgoing[me]
     others = pl.ds(0, owners - 1)
     for which in range(2):
@@ -299,11 +299,13 @@
     offset = lax.broadcasted_iota(jnp.int32, (cols, PATCH), 1) - lax.broadcasted_iota(
         jnp.int32, (cols, PATCH), 0
     )
+    group = 4
     many = group * CAP
     down = lax.broadcasted_iota(jnp.int32, (PATCH, many * rows), 0)
     lane = lax.broadcasted_iota(jnp.int32, (1, many * rows), 1)
 
     def gather(g, carry):
+        g = (g + owners // group // 2) % (owners // group)
         target = lane % rows
         shifted = []
         for n in range(group):

time: 51 us -> 49.2 us (0.965)
  Pallas kernels: 45.8 us -> 43.9 us
    pallas_call x1, Pallas kernels: 45.8 us -> 43.9 us  [shards(): pl.pallas_call(functools.partial(whole_kernel, nrow, ncol), out_shape=(tr...]
where the time goes in v4:
time: 49.2 us; the launch traced here: 48.9 us
  Pallas kernels  43.9 us (89%)
  local copies, waits for them, and re-layouts  3.67 us (7%)
  other arithmetic  0.68 us (1%)
  between operations  0.66 us (1%)
    pallas_call x1, Pallas kernels, shards(): pl.pallas_call(functools.partial(whole_kernel, nrow, ncol), out_shape=(tr...  43.9 us
    unnamed x6, local copies, waits for them, and re-layouts  3.45 us

profile of v4, /device:TPU:1, one launch (start us, length us, event | category | flops | bytes accessed | tf_op | source)
XLA Modules:
  0.0 48.9 jit_solution(8310599065474531834)
XLA Ops:
  0.6 0.0 copy-start.1
  0.6 0.6 %copy-done.1 = f32[31]{0:T(128)S(1)} copy-done((f32[31]{0:T(128)S(1)}, f32[31]{0:T(128)}, u32[]{:S(2)}) %copy-start.1) | copy-done | bytes 148
  1.3 0.1 pad_slice_fusion
  1.4 0.1 pad_slice_fusion.1
  1.4 0.1 pad_maximum_fusion.1
  1.5 0.1 pad.4
  1.6 0.6 %pad_maximum_fusion.taps = f32[2,512]{1,0:T(2,128)} fusion(f32[1,512]{1,0:T(1,128)S(1)} %bitcast.9, f32[1,512]{1,0:T(1,128)S(1)} %bitcast.10), kind=kLoop, calls=%fused_computation | loop fusion | flops 1024 | bytes 8192 | tf_op jit(solution)/shard_map/stack | solution.py:434
  2.2 43.9 %whole.1 = (f32[384,384]{1,0:T(8,128)}, f32[384,384]{1,0:T(8,128)}) custom-call(s32[1,64]{1,0:T(1,128)} %bitcast.12, s32[1,64]{1,0:T(1,128)} %bitcast.13, s32[1,64]{1,0:T(1,128)} %bitcast.14, s32[1,64]{1,0:T(1,128)} %bitcast.15, f32[1,256]{1,0:T(1,128)} %bitcast.11, f32[21,256]{1,0:T(8,128)} %bitcast.8, bf16[21,31]{1,0:T(8,128)(2,1)} %basis_rows.1, ...), custom_call_target="tpu_custom_call" | custom-call | tf_op jit(solution)/shard_map/whole/pallas_call | solution.py:437
  46.0 0.0 copy-start
  46.1 2.0 %copy.14 = f32[384,384]{1,0:T(8,128)} copy(f32[384,384]{1,0:T(8,128)} %get-tuple-element.4) | data formatting | bytes 1179648
  48.0 0.0 copy-done
  48.0 0.8 %copy.15 = f32[384,384]{1,0:T(8,128)} copy(f32[384,384]{1,0:T(8,128)S(1)} %copy-done) | data formatting | bytes 1179648
Async XLA Ops:
  0.6 0.7 %copy-start.1 = (f32[31]{0:T(128)S(1)}, f32[31]{0:T(128)}, u32[]{:S(2)}) copy-start(f32[31]{0:T(128)} %param.19) | copy-start | bytes 376
  46.0 2.0 %copy-start = (f32[384,384]{1,0:T(8,128)S(1)}, f32[384,384]{1,0:T(8,128)}, u32[]{:S(2)}) copy-start(f32[384,384]{1,0:T(8,128)} %get-tuple-element.5) | copy-start | bytes 1769476
